TPU v7x, 256 devices: a whole 4x4x8 slice. The times are simulated.
256 devices in a mesh: freq: 4 (over y_hi, core), slab: 64 (over y_lo, z, x).
Axes of the slice: x: 4, y: 4 (y_hi: 2, y_lo: 2; y = y_hi * 2 + y_lo), z: 8, core: 2. Of those that a mesh axis runs over, the one named last changes fastest.
Arguments:
- inverse_permittivity: float32 [512, 24, 512], P('slab'), may hold values from 0.083 to 1
- forward_fields: float32 [4, 6, 512, 24, 512], P('freq', None, 'slab'), may hold values from -6 to 6
- adjoint_fields: float32 [4, 6, 512, 24, 512], P('freq', None, 'slab'), may hold values from -6 to 6
- source_wave: float32 [4, 3], P('freq'), may hold values from -4 to 4
- source_profile: float32 [4, 512], P('freq'), may hold values from -4 to 4
- adjoint_wave: float32 [4, 3], P('freq'), may hold values from -4 to 4
- adjoint_profile: float32 [4, 512], P('freq'), may hold values from -4 to 4
- source_plane: int32 [4], P('freq'), may hold values from 0 to 23
- monitor_plane: int32 [4], P('freq'), may hold values from 0 to 23
- radius_map: int32 [64, 8], P('slab'), may hold values from 1 to 4
- design_mask: int32 [64, 8], P('slab'), may hold values 0 or 1
- design_density: float32 [512, 512], P('slab'), may hold values from 0 to 1
Outputs:
- forward_out: float32 [4, 6, 512, 24, 512], P('freq', None, 'slab')
- adjoint_out: float32 [4, 6, 512, 24, 512], P('freq', None, 'slab')
- projected: float32 [512, 512], P('slab')
Inputs may be any that keep to these rules, and one draw needn't show every extreme that they name: `radius_map`: filter radius of a tile in cells.
All inputs are finite; a program needn't handle non-finite values. No bound on the sum of `design_mask` on one device may be relied on, other than what follows from the above.
Results may differ from a plain program's by a relative error of at most 0.0003.
Values sent between devices are 32-bit elements; how exact they have to be, the bound alone decides.
A program may use at most 64 MiB of HBM per device.

v0:
```python
import math

import jax
import jax.numpy as jnp
from jax import lax
from jax.sharding import PartitionSpec as P

NY = 512
NZ = 24
FREQS = 4
STEPS = 3
RMAX = 4


courant = 0.5
sharpness = 4.0
midpoint = 0.5
step_size = 0.3


def shifted(shard, axis, by):
    length = lax.axis_size(axis)
    pairs = [(i, i + by) for i in range(length) if 0 <= i + by < length]
    return lax.ppermute(shard, axis, pairs)


def over_pieces(shard, axis):
    return lax.all_gather(shard, axis).sum(0)


def padded_2(cells, sides, width):
    for axis, dim in sides:
        count = lax.axis_size(axis)
        ends = count - 1
        head = lax.slice_in_dim(cells, 0, width, axis=dim)
        tail = lax.slice_in_dim(cells, cells.shape[dim] - width, cells.shape[dim], axis=dim)
        cells = jnp.concatenate(
            [
                lax.ppermute(tail, axis, [(i, (i + 1) % count) for i in range(ends)]),
                cells,
                lax.ppermute(head, axis, [((i + 1) % count, i) for i in range(ends)]),
            ],
            axis=dim,
        )
    return cells


def forward_cell(field, axis):
    axis = field.ndim + axis
    size = field.shape[axis]
    inner = lax.slice_in_dim(field, 1, size, axis=axis)
    edge = jnp.zeros_like(lax.slice_in_dim(field, 0, 1, axis=axis))
    return jnp.concatenate([inner, edge], axis=axis)


def backward_cell(field, axis):
    axis = field.ndim + axis
    size = field.shape[axis]
    inner = lax.slice_in_dim(field, 0, size - 1, axis=axis)
    edge = jnp.zeros_like(lax.slice_in_dim(field, 0, 1, axis=axis))
    return jnp.concatenate([edge, inner], axis=axis)


def next_rows(field, plane):
    return jnp.concatenate([field[:, :, 1:], plane[:, :, None]], axis=2)


def prior_rows(field, plane):
    return jnp.concatenate([plane[:, :, None], field[:, :, :-1]], axis=2)


def send_electric(first, second):
    planes = shifted(jnp.stack([first[:, :, 0], second[:, :, 0]]), "slab", -1)
    return (planes[0], planes[1])


def send_magnetic(first, second):
    planes = shifted(jnp.stack([first[:, :, -1], second[:, :, -1]]), "slab", 1)
    return (planes[0], planes[1])


def yee_update(fields, inverse, source, electric_planes, magnetic_planes):
    elec_x, elec_y, elec_z, magn_x, magn_y, magn_z = fields
    next_y, next_z = electric_planes(elec_y, elec_z)
    magn_x = magn_x - courant * (
        forward_cell(elec_z, -1) - elec_z - (forward_cell(elec_y, -2) - elec_y)
    )
    magn_y = magn_y - courant * (
        forward_cell(elec_x, -2) - elec_x - (next_rows(elec_z, next_z) - elec_z)
    )
    magn_z = magn_z - courant * (
        next_rows(elec_y, next_y) - elec_y - (forward_cell(elec_x, -1) - elec_x)
    )
    prior_y, prior_z = magnetic_planes(magn_y, magn_z)
    elec_x = (
        elec_x
        + courant
        * inverse
        * (magn_z - backward_cell(magn_z, -1) - (magn_y - backward_cell(magn_y, -2)))
        + source
    )
    elec_y = elec_y + courant * inverse * (
        magn_x - backward_cell(magn_x, -2) - (magn_z - prior_rows(magn_z, prior_z))
    )
    elec_z = elec_z + courant * inverse * (
        magn_y - prior_rows(magn_y, prior_y) - (magn_x - backward_cell(magn_x, -1))
    )
    return (elec_x, elec_y, elec_z, magn_x, magn_y, magn_z)


def intersection_of(fields):
    total = 0.0
    for component in range(3):
        part = fields[component]
        total = total + part[0] * part[1]
    return jnp.sum(total, axis=2)


def on_device(
    inverse_permittivity,
    forward_fields,
    adjoint_fields,
    source_wave,
    source_profile,
    adjoint_wave,
    adjoint_profile,
    source_plane,
    monitor_plane,
    radius_map,
    design_mask,
    design_density,
):
    groups = forward_fields.shape[0]
    rows = forward_fields.shape[2]
    waves = jnp.stack([source_wave, adjoint_wave])
    profiles = jnp.stack([source_profile, adjoint_profile])
    planes = jnp.stack([source_plane, monitor_plane])
    plane_hit = (jnp.arange(NZ, dtype=jnp.int32)[None, None, :] == planes[:, :, None]).astype(
        jnp.float32
    )
    state = jnp.stack([forward_fields, adjoint_fields])
    intersection = jnp.zeros((groups, rows, NY), jnp.float32)
    fields = tuple((state[:, :, component] for component in range(6)))
    for turn in range(STEPS):
        source = (
            waves[:, :, turn][:, :, None, None, None]
            * plane_hit[:, :, None, :, None]
            * profiles[:, :, None, None, :]
        )
        fields = yee_update(fields, inverse_permittivity, source, send_electric, send_magnetic)
        intersection = intersection + intersection_of(fields)
    forward_out = jnp.stack([member[0] for member in fields], axis=1)
    adjoint_out = jnp.stack([member[1] for member in fields], axis=1)
    local = jnp.sum(intersection, axis=0)
    sent = over_pieces(local, "freq").T
    tiles = lax.all_to_all(sent, "slab", split_axis=0, concat_axis=1, tiled=True)
    tile_rows = tiles.shape[0]
    width = design_density.shape[1]
    columns = width // radius_map.shape[1]
    radius = jnp.repeat(radius_map, columns, axis=1).astype(jnp.float32)
    chosen = jnp.repeat(design_mask, columns, axis=1).astype(jnp.float32)
    scale = step_size / math.sqrt(3 * STEPS * NZ * FREQS)
    updated = design_density + scale * chosen * tiles
    rim = padded_2(updated, (("slab", 0),), RMAX)
    padded = jnp.pad(rim, ((0, 0), (RMAX, RMAX)))
    global_y = (
        lax.axis_index("slab") * tile_rows
        - RMAX
        + jnp.arange(tile_rows + 2 * RMAX, dtype=jnp.int32)
    )
    inside_y = ((global_y >= 0) & (global_y < NY)).astype(jnp.float32)
    inside_x = jnp.pad(jnp.ones((width,), jnp.float32), RMAX)
    inside = inside_y[:, None] * inside_x[None, :]
    numerator = jnp.zeros((tile_rows, width), jnp.float32)
    weight_total = jnp.zeros((tile_rows, width), jnp.float32)
    for offset_y in range(2 * RMAX + 1):
        for offset_x in range(2 * RMAX + 1):
            distance = jnp.sqrt(
                jnp.asarray((offset_y - RMAX) ** 2 + (offset_x - RMAX) ** 2, jnp.float32)
            )
            weight = jnp.maximum(radius - distance, 0.0)
            piece = padded[offset_y : offset_y + tile_rows, offset_x : offset_x + width]
            present = inside[offset_y : offset_y + tile_rows, offset_x : offset_x + width]
            numerator = numerator + weight * present * piece
            weight_total = weight_total + weight * present
    filtered = numerator / weight_total
    base = math.tanh(sharpness * midpoint)
    projected = (base + jnp.tanh(sharpness * (filtered - midpoint))) / (
        base + math.tanh(sharpness * (1.0 - midpoint))
    )
    return (forward_out, adjoint_out, projected)


def solution(mesh):
    return jax.shard_map(
        on_device,
        mesh=mesh,
        in_specs=(
            P("slab", None, None),
            P("freq", None, "slab", None, None),
            P("freq", None, "slab", None, None),
            P("freq", None),
            P("freq", None),
            P("freq", None),
            P("freq", None),
            P("freq"),
            P("freq"),
            P("slab", None),
            P("slab", None),
            P("slab", None),
        ),
        out_specs=(
            P("freq", None, "slab", None, None),
            P("freq", None, "slab", None, None),
            P("slab", None),
        ),
        check_vma=False,
    )
```

profile of v0, /device:TPU:6, one launch (start us, length us, event | category | flops | bytes accessed | tf_op | source)
XLA Modules:
  0.0 145.0 jit_solution(11330417361804338812)
XLA Ops:
  0.6 1.9 %fusion.9 = (f32[2,1,8,24,512]{4,3,0,2,1:T(8,128)S(1)}, f32[2,1,8,24,512]{4,3,0,2,1:T(8,128)S(1)}, f32[2,1,8,24,512]{4,3,0,2,1:T(8,128)S(1)}) fusion(f32[1,1,6,8,24,512]{5,4,0,3,2,1:T(8,128)} %bitcast.156, f32[1,1,6,8,24,512]{5,4,0,3,2,1:T(8,128)} %bitcast.158), kind=kLoop, calls=%fused_computation.19 | loop fusion | flops 589824 | bytes 7077888 | tf_op jit(solution)/shard_map/squeeze | solution.py:143
  3.2 2.7 %collective-permute-start = (f32[2,2,1,24,512]{4,3,1,2,0:T(8,128)}, f32[2,2,1,24,512]{4,3,1,2,0:T(8,128)}, u32[]{:S(2)}, u32[]{:S(2)}) collective-permute-start(f32[2,2,1,24,512]{4,3,1,2,0:T(8,128)} %pad_maximum_fusion.1), channel_id=1, source_target_pairs={{1,0},{2,1},{3,2},{4,3},{5,4},{6,5},{7,6},{8,7},{9,8},{10,9},{11,1... | collective-permute-start | bytes 589832 | tf_op jit(solution)/shard_map/ppermute | solution.py:24
  13.4 1.3 maximum_bitcast_fusion.15
  35.4 3.9 %fusion.13 = (f32[2,1,8,24,512]{4,3,0,2,1:T(8,128)S(1)}, f32[2,1,8,24,512]{4,3,0,2,1:T(8,128)S(1)}, f32[2,1,8,24,512]{4,3,0,2,1:T(8,128)S(1)}) fusion(f32[1,1,6,8,24,512]{5,4,0,3,2,1:T(8,128)} %bitcast.159, f32[1,1,6,8,24,512]{5,4,0,3,2,1:T(8,128)} %bitcast.157, f32[2,1,8,24,512]{4,3,0,2,1:T(8,128)S(1)} %get-tuple-element.9, ...), kind=kLoop, calls=%fused_computation.24 | loop fusion | flops 3932160 | bytes 14087168 | tf_op jit(solution)/shard_map/sub | solution.py:85
  39.4 5.2 %collective-permute-start.1 = (f32[2,2,1,24,512]{4,3,1,2,0:T(8,128)S(1)}, f32[2,2,1,24,512]{4,3,1,2,0:T(8,128)S(1)}, u32[]{:S(2)}, u32[]{:S(2)}) collective-permute-start(f32[2,2,1,24,512]{4,3,1,2,0:T(8,128)S(1)} %pad_maximum_fusion.2), channel_id=1, source_target_pairs={{0,1},{1,2},{2,3},{3,4},{4,5},{5,6},{6,7},{7,8},{8,9},{9,10},{10,1... | collective-permute-start | bytes 589832 | tf_op jit(solution)/shard_map/ppermute | solution.py:24
  44.8 3.7 %collective-permute-done.1 = f32[2,2,1,24,512]{4,3,1,2,0:T(8,128)S(1)} collective-permute-done((f32[2,2,1,24,512]{4,3,1,2,0:T(8,128)S(1)}, f32[2,2,1,24,512]{4,3,1,2,0:T(8,128)S(1)}, u32[]{:S(2)}, u32[]{:S(2)}) %collective-permute-start.1) | collective-permute-done | bytes 196640 | tf_op jit(solution)/shard_map/ppermute | solution.py:24
  48.5 1.5 %fusion.20 = (f32[2,1,8,24,512]{4,3,0,2,1:T(8,128)S(1)}, f32[2,1,8,24,512]{4,3,0,2,1:T(8,128)S(1)}, f32[2,1,8,24,512]{4,3,0,2,1:T(8,128)S(1)}) fusion(f32[2,1,8,24,512]{4,3,0,2,1:T(8,128)S(1)} %get-tuple-element.9, f32[2,1,8,24,512]{4,3,0,2,1:T(8,128)S(1)} %get-tuple-element.7, f32[2,1,7,24,512]{4,3,0,2,1:T(8,128)S(1)} %slice.1076, ...), kind=kLoop, calls=%fused_computation.34 | loop fusion | flops 3538944 | bytes 12219392 | tf_op jit(solution)/shard_map/add | solution.py:102
  50.0 1.9 %collective-permute-start.2 = (f32[2,2,1,24,512]{4,3,1,2,0:T(8,128)S(1)}, f32[2,2,1,24,512]{4,3,1,2,0:T(8,128)S(1)}, u32[]{:S(2)}, u32[]{:S(2)}) collective-permute-start(f32[2,2,1,24,512]{4,3,1,2,0:T(8,128)S(1)} %pad_maximum_fusion.3), channel_id=1, source_target_pairs={{1,0},{2,1},{3,2},{4,3},{5,4},{6,5},{7,6},{8,7},{9,8},{10,9},{11,1... | collective-permute-start | bytes 589832 | tf_op jit(solution)/shard_map/ppermute | solution.py:24
  52.9 7.4 %collective-permute-done.2 = f32[2,2,1,24,512]{4,3,1,2,0:T(8,128)S(1)} collective-permute-done((f32[2,2,1,24,512]{4,3,1,2,0:T(8,128)S(1)}, f32[2,2,1,24,512]{4,3,1,2,0:T(8,128)S(1)}, u32[]{:S(2)}, u32[]{:S(2)}) %collective-permute-start.2) | collective-permute-done | bytes 196640 | tf_op jit(solution)/shard_map/ppermute | solution.py:24
  61.6 3.8 %collective-permute-start.3 = (f32[2,2,1,24,512]{4,3,1,2,0:T(8,128)S(1)}, f32[2,2,1,24,512]{4,3,1,2,0:T(8,128)S(1)}, u32[]{:S(2)}, u32[]{:S(2)}) collective-permute-start(f32[2,2,1,24,512]{4,3,1,2,0:T(8,128)S(1)} %pad_maximum_fusion.4), channel_id=1, source_target_pairs={{0,1},{1,2},{2,3},{3,4},{4,5},{5,6},{6,7},{7,8},{8,9},{9,10},{10,1... | collective-permute-start | bytes 589832 | tf_op jit(solution)/shard_map/ppermute | solution.py:24
  65.6 3.6 %collective-permute-done.3 = f32[2,2,1,24,512]{4,3,1,2,0:T(8,128)S(1)} collective-permute-done((f32[2,2,1,24,512]{4,3,1,2,0:T(8,128)S(1)}, f32[2,2,1,24,512]{4,3,1,2,0:T(8,128)S(1)}, u32[]{:S(2)}, u32[]{:S(2)}) %collective-permute-start.3) | collective-permute-done | bytes 196640 | tf_op jit(solution)/shard_map/ppermute | solution.py:24
  70.8 1.9 %collective-permute-start.4 = (f32[2,2,1,24,512]{4,3,1,2,0:T(8,128)S(1)}, f32[2,2,1,24,512]{4,3,1,2,0:T(8,128)S(1)}, u32[]{:S(2)}, u32[]{:S(2)}) collective-permute-start(f32[2,2,1,24,512]{4,3,1,2,0:T(8,128)S(1)} %pad_maximum_fusion.5), channel_id=1, source_target_pairs={{1,0},{2,1},{3,2},{4,3},{5,4},{6,5},{7,6},{8,7},{9,8},{10,9},{11,1... | collective-permute-start | bytes 589832 | tf_op jit(solution)/shard_map/ppermute | solution.py:24
  73.6 6.9 %collective-permute-done.4 = f32[2,2,1,24,512]{4,3,1,2,0:T(8,128)S(1)} collective-permute-done((f32[2,2,1,24,512]{4,3,1,2,0:T(8,128)S(1)}, f32[2,2,1,24,512]{4,3,1,2,0:T(8,128)S(1)}, u32[]{:S(2)}, u32[]{:S(2)}) %collective-permute-start.4) | collective-permute-done | bytes 196640 | tf_op jit(solution)/shard_map/ppermute | solution.py:24
  81.7 4.0 %collective-permute-start.5 = (f32[2,2,1,24,512]{4,3,1,2,0:T(8,128)S(1)}, f32[2,2,1,24,512]{4,3,1,2,0:T(8,128)S(1)}, u32[]{:S(2)}, u32[]{:S(2)}) collective-permute-start(f32[2,2,1,24,512]{4,3,1,2,0:T(8,128)S(1)} %pad_maximum_fusion.6), channel_id=1, source_target_pairs={{0,1},{1,2},{2,3},{3,4},{4,5},{5,6},{6,7},{7,8},{8,9},{9,10},{10,1... | collective-permute-start | bytes 589832 | tf_op jit(solution)/shard_map/ppermute | solution.py:24
  86.4 2.9 %collective-permute-done.5 = f32[2,2,1,24,512]{4,3,1,2,0:T(8,128)S(1)} collective-permute-done((f32[2,2,1,24,512]{4,3,1,2,0:T(8,128)S(1)}, f32[2,2,1,24,512]{4,3,1,2,0:T(8,128)S(1)}, u32[]{:S(2)}, u32[]{:S(2)}) %collective-permute-start.5) | collective-permute-done | bytes 196640 | tf_op jit(solution)/shard_map/ppermute | solution.py:24
  89.3 1.5 %fusion.43 = (f32[2,1,8,24,512]{4,3,2,1,0:T(8,128)S(1)}, f32[2,1,8,24,512]{4,3,2,1,0:T(8,128)S(1)}, f32[2,1,8,24,512]{4,3,2,1,0:T(8,128)S(1)}) fusion(f32[2,1,8,24,512]{4,3,2,1,0:T(8,128)S(1)} %get-tuple-element.16, f32[2,1,8,24,512]{4,3,2,1,0:T(8,128)S(1)} %get-tuple-element.34, f32[2,1,7,24,512]{4,3,2,1,0:T(8,128)S(1)} %slice.1122, ...), kind=kLoop, calls=%fused_computation.66 | loop fusion | flops 3735552 | bytes 12317696 | tf_op jit(solution)/shard_map/add | solution.py:105
  92.9 6.7 %all-gather = f32[32,512]{1,0:T(8,128)S(1)} all-gather(f32[8,512]{1,0:T(8,128)S(1)} %add_add_fusion.2), channel_id=2, replica_groups=mesh['freq'=4,'slab'=64] {'freq'}, dimensions={0}, use_global_device_ids=true | all-gather | bytes 81920 | tf_op jit(solution)/shard_map/all_gather | solution.py:28
  100.7 18.0 %all-to-all-start = ((f32[64,8,8]{1,2,0:T(8,128)}), f32[64,8,8]{1,2,0:T(8,128)S(1)}, u32[]{:S(2)}, u32[]{:S(2)}) async-start(f32[64,8,8]{1,2,0:T(8,128)} %copy.130), calls=%async_computation | async-start | bytes 524288 | tf_op jit(solution)/shard_map/all_to_all | solution.py:156
  118.7 2.1 %slice_dynamic-update-slice_fusion.7 = (f32[1,6,8,24,512]{4,3,2,1,0:T(8,128)}, f32[1,6,8,24,512]{4,3,2,1,0:T(8,128)}) fusion(f32[1,6,8,24,512]{4,3,2,1,0:T(8,128)} %get-tuple-element.21, f32[2,1,8,24,512]{4,3,2,1,0:T(8,128)} %copy-done, f32[1,6,8,24,512]{4,3,2,1,0:T(8,128)} %get-tuple-element.22), kind=kLoop, calls=%fused_computation.98 | loop fusion | bytes 1572864
  123.6 8.1 %all-to-all-done = f32[64,8,8]{1,2,0:T(8,128)S(1)} async-done(((f32[64,8,8]{1,2,0:T(8,128)}), f32[64,8,8]{1,2,0:T(8,128)S(1)}, u32[]{:S(2)}, u32[]{:S(2)}) %all-to-all-start) | async-done | bytes 16416 | tf_op jit(solution)/shard_map/all_to_all | solution.py:156
  131.9 3.9 %collective-permute-start.6 = (f32[4,512]{1,0:T(4,128)S(1)}, f32[4,512]{1,0:T(4,128)S(1)}, u32[]{:S(2)}, u32[]{:S(2)}) collective-permute-start(f32[4,512]{1,0:T(4,128)S(1)} %get-tuple-element.53), channel_id=1, source_target_pairs={{0,1},{1,2},{2,3},{3,4},{4,5},{5,6},{6,7},{7,8},{8,9},{9,10},{10,1... | collective-permute-start | bytes 24584 | tf_op jit(solution)/shard_map/ppermute | solution.py:39
  135.8 1.9 %collective-permute-start.7 = (f32[4,512]{1,0:T(4,128)S(1)}, f32[4,512]{1,0:T(4,128)S(1)}, u32[]{:S(2)}, u32[]{:S(2)}) collective-permute-start(f32[4,512]{1,0:T(4,128)S(1)} %get-tuple-element.54), channel_id=1, source_target_pairs={{1,0},{2,1},{3,2},{4,3},{5,4},{6,5},{7,6},{8,7},{9,8},{10,9},{11,1... | collective-permute-start | bytes 24584 | tf_op jit(solution)/shard_map/ppermute | solution.py:41
  138.7 4.8 %collective-permute-done.7 = f32[4,512]{1,0:T(4,128)S(1)} collective-permute-done((f32[4,512]{1,0:T(4,128)S(1)}, f32[4,512]{1,0:T(4,128)S(1)}, u32[]{:S(2)}, u32[]{:S(2)}) %collective-permute-start.7) | collective-permute-done | bytes 8224 | tf_op jit(solution)/shard_map/ppermute | solution.py:41
  143.7 1.3 add_multiply_fusion
  (150 shorter events, 41.5 us)
Async XLA Ops:
  3.2 31.2 %collective-permute-start = (f32[2,2,1,24,512]{4,3,1,2,0:T(8,128)}, f32[2,2,1,24,512]{4,3,1,2,0:T(8,128)}, u32[]{:S(2)}, u32[]{:S(2)}) collective-permute-start(f32[2,2,1,24,512]{4,3,1,2,0:T(8,128)} %pad_maximum_fusion.1), channel_id=1, source_target_pairs={{1,0},{2,1},{3,2},{4,3},{5,4},{6,5},{7,6},{8,7},{9,8},{10,9},{11,1... | collective-permute-start | bytes 589832 | tf_op jit(solution)/shard_map/ppermute | solution.py:24
  8.0 24.5 %copy-start.1 = (f32[8,24,512]{2,1,0:T(8,128)S(1)}, f32[8,24,512]{2,1,0:T(8,128)}, u32[]{:S(2)}) copy-start(f32[8,24,512]{2,1,0:T(8,128)} %param.12) | copy-start | bytes 1179652
  39.4 9.1 %collective-permute-start.1 = (f32[2,2,1,24,512]{4,3,1,2,0:T(8,128)S(1)}, f32[2,2,1,24,512]{4,3,1,2,0:T(8,128)S(1)}, u32[]{:S(2)}, u32[]{:S(2)}) collective-permute-start(f32[2,2,1,24,512]{4,3,1,2,0:T(8,128)S(1)} %pad_maximum_fusion.2), channel_id=1, source_target_pairs={{0,1},{1,2},{2,3},{3,4},{4,5},{5,6},{6,7},{7,8},{8,9},{9,10},{10,1... | collective-permute-start | bytes 589832 | tf_op jit(solution)/shard_map/ppermute | solution.py:24
  50.0 10.3 %collective-permute-start.2 = (f32[2,2,1,24,512]{4,3,1,2,0:T(8,128)S(1)}, f32[2,2,1,24,512]{4,3,1,2,0:T(8,128)S(1)}, u32[]{:S(2)}, u32[]{:S(2)}) collective-permute-start(f32[2,2,1,24,512]{4,3,1,2,0:T(8,128)S(1)} %pad_maximum_fusion.3), channel_id=1, source_target_pairs={{1,0},{2,1},{3,2},{4,3},{5,4},{6,5},{7,6},{8,7},{9,8},{10,9},{11,1... | collective-permute-start | bytes 589832 | tf_op jit(solution)/shard_map/ppermute | solution.py:24
  61.6 7.6 %collective-permute-start.3 = (f32[2,2,1,24,512]{4,3,1,2,0:T(8,128)S(1)}, f32[2,2,1,24,512]{4,3,1,2,0:T(8,128)S(1)}, u32[]{:S(2)}, u32[]{:S(2)}) collective-permute-start(f32[2,2,1,24,512]{4,3,1,2,0:T(8,128)S(1)} %pad_maximum_fusion.4), channel_id=1, source_target_pairs={{0,1},{1,2},{2,3},{3,4},{4,5},{5,6},{6,7},{7,8},{8,9},{9,10},{10,1... | collective-permute-start | bytes 589832 | tf_op jit(solution)/shard_map/ppermute | solution.py:24
  70.8 9.7 %collective-permute-start.4 = (f32[2,2,1,24,512]{4,3,1,2,0:T(8,128)S(1)}, f32[2,2,1,24,512]{4,3,1,2,0:T(8,128)S(1)}, u32[]{:S(2)}, u32[]{:S(2)}) collective-permute-start(f32[2,2,1,24,512]{4,3,1,2,0:T(8,128)S(1)} %pad_maximum_fusion.5), channel_id=1, source_target_pairs={{1,0},{2,1},{3,2},{4,3},{5,4},{6,5},{7,6},{8,7},{9,8},{10,9},{11,1... | collective-permute-start | bytes 589832 | tf_op jit(solution)/shard_map/ppermute | solution.py:24
  81.7 7.6 %collective-permute-start.5 = (f32[2,2,1,24,512]{4,3,1,2,0:T(8,128)S(1)}, f32[2,2,1,24,512]{4,3,1,2,0:T(8,128)S(1)}, u32[]{:S(2)}, u32[]{:S(2)}) collective-permute-start(f32[2,2,1,24,512]{4,3,1,2,0:T(8,128)S(1)} %pad_maximum_fusion.6), channel_id=1, source_target_pairs={{0,1},{1,2},{2,3},{3,4},{4,5},{5,6},{6,7},{7,8},{8,9},{9,10},{10,1... | collective-permute-start | bytes 589832 | tf_op jit(solution)/shard_map/ppermute | solution.py:24
  100.7 31.1 %all-to-all-start = ((f32[64,8,8]{1,2,0:T(8,128)}), f32[64,8,8]{1,2,0:T(8,128)S(1)}, u32[]{:S(2)}, u32[]{:S(2)}) async-start(f32[64,8,8]{1,2,0:T(8,128)} %copy.130), calls=%async_computation | async-start | bytes 524288 | tf_op jit(solution)/shard_map/all_to_all | solution.py:156
  120.8 11.1 %copy-start.2 = (f32[8,512]{1,0:T(8,128)S(1)}, f32[8,512]{1,0:T(8,128)}, u32[]{:S(2)}) copy-start(f32[8,512]{1,0:T(8,128)} %param.23) | copy-start | bytes 49156
  121.7 21.9 %copy-start.3 = (f32[512]{0:T(512)S(1)}, f32[512]{0:T(512)}, u32[]{:S(2)}) copy-start(f32[512]{0:T(512)} %max.299) | copy-start | bytes 6148
  121.7 21.9 %copy-start.4 = (f32[512]{0:T(512)S(1)}, f32[512]{0:T(512)}, u32[]{:S(2)}) copy-start(f32[512]{0:T(512)} %max.302) | copy-start | bytes 6148
  121.7 21.9 %copy-start.5 = (f32[512]{0:T(512)S(1)}, f32[512]{0:T(512)}, u32[]{:S(2)}) copy-start(f32[512]{0:T(512)} %max.305) | copy-start | bytes 6148
  121.7 21.9 %copy-start.6 = (f32[512]{0:T(512)S(1)}, f32[512]{0:T(512)}, u32[]{:S(2)}) copy-start(f32[512]{0:T(512)} %max.308) | copy-start | bytes 6148
  121.7 21.9 %copy-start.7 = (f32[512]{0:T(512)S(1)}, f32[512]{0:T(512)}, u32[]{:S(2)}) copy-start(f32[512]{0:T(512)} %max.311) | copy-start | bytes 6148
  121.7 21.9 %copy-start.8 = (f32[512]{0:T(512)S(1)}, f32[512]{0:T(512)}, u32[]{:S(2)}) copy-start(f32[512]{0:T(512)} %max.314) | copy-start | bytes 6148
  121.7 21.9 %copy-start.9 = (f32[512]{0:T(512)S(1)}, f32[512]{0:T(512)}, u32[]{:S(2)}) copy-start(f32[512]{0:T(512)} %max.317) | copy-start | bytes 6148
  121.7 21.9 %copy-start.10 = (f32[512]{0:T(512)S(1)}, f32[512]{0:T(512)}, u32[]{:S(2)}) copy-start(f32[512]{0:T(512)} %max.320) | copy-start | bytes 6148
  121.7 21.9 %copy-start.11 = (f32[512]{0:T(512)S(1)}, f32[512]{0:T(512)}, u32[]{:S(2)}) copy-start(f32[512]{0:T(512)} %max.323) | copy-start | bytes 6148
  121.7 21.9 %copy-start.12 = (f32[512]{0:T(512)S(1)}, f32[512]{0:T(512)}, u32[]{:S(2)}) copy-start(f32[512]{0:T(512)} %max.326) | copy-start | bytes 6148
  121.8 21.9 %copy-start.13 = (f32[512]{0:T(512)S(1)}, f32[512]{0:T(512)}, u32[]{:S(2)}) copy-start(f32[512]{0:T(512)} %max.329) | copy-start | bytes 6148
  121.8 21.9 %copy-start.14 = (f32[512]{0:T(512)S(1)}, f32[512]{0:T(512)}, u32[]{:S(2)}) copy-start(f32[512]{0:T(512)} %max.332) | copy-start | bytes 6148
  121.8 21.9 %copy-start.15 = (f32[512]{0:T(512)S(1)}, f32[512]{0:T(512)}, u32[]{:S(2)}) copy-start(f32[512]{0:T(512)} %max.335) | copy-start | bytes 6148
  131.9 6.8 %collective-permute-start.6 = (f32[4,512]{1,0:T(4,128)S(1)}, f32[4,512]{1,0:T(4,128)S(1)}, u32[]{:S(2)}, u32[]{:S(2)}) collective-permute-start(f32[4,512]{1,0:T(4,128)S(1)} %get-tuple-element.53), channel_id=1, source_target_pairs={{0,1},{1,2},{2,3},{3,4},{4,5},{5,6},{6,7},{7,8},{8,9},{9,10},{10,1... | collective-permute-start | bytes 24584 | tf_op jit(solution)/shard_map/ppermute | solution.py:39
  135.8 7.7 %collective-permute-start.7 = (f32[4,512]{1,0:T(4,128)S(1)}, f32[4,512]{1,0:T(4,128)S(1)}, u32[]{:S(2)}, u32[]{:S(2)}) collective-permute-start(f32[4,512]{1,0:T(4,128)S(1)} %get-tuple-element.54), channel_id=1, source_target_pairs={{1,0},{2,1},{3,2},{4,3},{5,4},{6,5},{7,6},{8,7},{9,8},{10,9},{11,1... | collective-permute-start | bytes 24584 | tf_op jit(solution)/shard_map/ppermute | solution.py:41
  (3 other events, 9.6 us)
where the time goes:
time: 146 us; the launch traced here: 145 us
  starting transfers between devices  43.4 us (30%)
  waiting for transfers between devices  37.3 us (26%)
  local copies, waits for them, and re-layouts  34.4 us (24%)
  other arithmetic  20.4 us (14%)
  blocking collectives  6.72 us (5%)
  between operations  2.64 us (2%)
    ppermute x6, waiting for transfers between devices, shifted(): return lax.ppermute(shard, axis, pairs)  24.4 us
    ppermute x6, starting transfers between devices, shifted(): return lax.ppermute(shard, axis, pairs)  19.6 us
    all_to_all x1, starting transfers between devices, on_device(): lax.all_to_all(sent, 'slab', split_axis=0, concat_axis=1, tiled=True)  18 us
    broadcast_in_dim x15, local copies, waits for them, and re-layouts, on_device(): radius = jnp.repeat(radius_map, columns, axis=1).astype(jnp.float32)  9.18 us
    max x15, local copies, waits for them, and re-layouts, on_device(): weight = jnp.maximum(radius - distance, 0.0)  8.66 us
    all_to_all x1, waiting for transfers between devices, on_device(): lax.all_to_all(sent, 'slab', split_axis=0, concat_axis=1, tiled=True)  8.12 us
    all_gather x1, blocking collectives, over_pieces(): return lax.all_gather(shard, axis).sum(0)  6.72 us
    unnamed x40, local copies, waits for them, and re-layouts  5.81 us
  transfers between devices with their start and end apart: 9, of which 7 were waited for; matrix products, arithmetic and copies ran while one was open for 25% of the time, Pallas kernels for 0%

commit v1 on v0

v1 whole, which is shorter than its diff:
```python
import math

import jax
import jax.numpy as jnp
from jax import lax
from jax.experimental import pallas as pl
from jax.experimental.pallas import tpu as pltpu
from jax.sharding import PartitionSpec as P

NY = 512
NZ = 24
FREQS = 4
STEPS = 3
RMAX = 4


courant = 0.5
sharpness = 4.0
midpoint = 0.5
step_size = 0.3


def next_y(v):
    lane = lax.broadcasted_iota(jnp.int32, v.shape, 1)
    return jnp.where(lane == v.shape[1] - 1, 0.0, pltpu.roll(v, v.shape[1] - 1, 1))


def prior_y(v):
    lane = lax.broadcasted_iota(jnp.int32, v.shape, 1)
    return jnp.where(lane == 0, 0.0, pltpu.roll(v, 1, 1))


def next_z(v):
    row = lax.broadcasted_iota(jnp.int32, v.shape, 0)
    return jnp.where(row == v.shape[0] - 1, 0.0, pltpu.roll(v, v.shape[0] - 1, 0))


def prior_z(v):
    row = lax.broadcasted_iota(jnp.int32, v.shape, 0)
    return jnp.where(row == 0, 0.0, pltpu.roll(v, 1, 0))


def yee_kernel(
    inverse_hbm, forward_hbm, adjoint_hbm, swave_hbm, sprofile_hbm, awave_hbm, aprofile_hbm, splane_hbm, mplane_hbm,
    forward_out, adjoint_out, local_out,
    state, inverse, waves, profiles, planes, sources, partial, ghost_e, ghost_p, acc, local,
    load_sem, small_sem, e_send, e_recv, p_send, p_recv, out_sem,
):
    count = lax.axis_size("slab")
    me = lax.axis_index("slab")
    right, left = lax.rem(me + 1, count), lax.rem(me + count - 1, count)
    is_last = me == count - 1
    is_first = me == 0
    rows = state.shape[2]
    top = rows - 1
    c = courant

    barrier = pltpu.get_barrier_semaphore()
    for neighbour in (left, right):
        pl.semaphore_signal(
            barrier, inc=1, device_id={"slab": neighbour}, device_id_type=pl.DeviceIdType.MESH
        )

    loads = [
        pltpu.make_async_copy(forward_hbm.at[0], state.at[0], load_sem.at[0]),
        pltpu.make_async_copy(adjoint_hbm.at[0], state.at[1], load_sem.at[1]),
        pltpu.make_async_copy(inverse_hbm, inverse, load_sem.at[2]),
    ]
    smalls = [
        pltpu.make_async_copy(swave_hbm, waves.at[0], small_sem.at[0]),
        pltpu.make_async_copy(awave_hbm, waves.at[1], small_sem.at[1]),
        pltpu.make_async_copy(sprofile_hbm, profiles.at[0], small_sem.at[2]),
        pltpu.make_async_copy(aprofile_hbm, profiles.at[1], small_sem.at[3]),
        pltpu.make_async_copy(splane_hbm, planes.at[0], small_sem.at[4]),
        pltpu.make_async_copy(mplane_hbm, planes.at[1], small_sem.at[5]),
    ]
    for copy in loads + smalls:
        copy.start()

    def send_e(run, turn):
        return pltpu.make_async_remote_copy(
            src_ref=state.at[run, pl.ds(1, 2), 0],
            dst_ref=ghost_e.at[turn, run],
            send_sem=e_send.at[turn, run],
            recv_sem=e_recv.at[turn, run],
            device_id={"slab": left},
            device_id_type=pl.DeviceIdType.MESH,
        )

    def send_p(run, turn):
        return pltpu.make_async_remote_copy(
            src_ref=partial.at[turn, run],
            dst_ref=ghost_p.at[turn, run],
            send_sem=p_send.at[turn, run],
            recv_sem=p_recv.at[turn, run],
            device_id={"slab": right},
            device_id_type=pl.DeviceIdType.MESH,
        )

    def make_partial(run, turn):
        elec_x, elec_y, elec_z = (state[run, comp, top] for comp in range(3))
        partial[turn, run, 0] = state[run, 4, top] - c * (next_z(elec_x) - elec_x + elec_z)
        partial[turn, run, 1] = state[run, 5, top] + c * (elec_y + next_y(elec_x) - elec_x)

    def magnetic_x(run, row):
        elec_y, elec_z = state[run, 1, row], state[run, 2, row]
        state[run, 3, row] = state[run, 3, row] - c * (
            next_y(elec_z) - elec_z - (next_z(elec_y) - elec_y)
        )

    def magnetic_row(run, row):
        magnetic_x(run, row)
        elec_x, elec_y, elec_z = (state[run, comp, row] for comp in range(3))
        state[run, 4, row] = state[run, 4, row] - c * (
            next_z(elec_x) - elec_x - (state[run, 2, row + 1] - elec_z)
        )
        state[run, 5, row] = state[run, 5, row] - c * (
            state[run, 1, row + 1] - elec_y - (next_y(elec_x) - elec_x)
        )

    def electric_row(run, row, turn, prior_hy, prior_hz):
        magn_x, magn_y, magn_z = (state[run, comp, row] for comp in range(3, 6))
        scaled = c * inverse[row]
        source = sources[run] * waves[run, :, turn : turn + 1]
        elec_x = (
            state[run, 0, row]
            + scaled * (magn_z - prior_y(magn_z) - (magn_y - prior_z(magn_y)))
            + source
        )
        elec_y = state[run, 1, row] + scaled * (magn_x - prior_z(magn_x) - (magn_z - prior_hz))
        elec_z = state[run, 2, row] + scaled * (magn_y - prior_hy - (magn_x - prior_y(magn_x)))
        state[run, 0, row] = elec_x
        state[run, 1, row] = elec_y
        state[run, 2, row] = elec_z
        if run == 1:
            total = (
                elec_x * state[0, 0, row] + elec_y * state[0, 1, row] + elec_z * state[0, 2, row]
            )
            folded = total[0:8] + total[8:16] + total[16:24]
            if turn == 0:
                acc[row] = folded
            else:
                acc[row] = acc[row] + folded

    def interior(run, turn):
        magnetic_row(run, 0)

        @pl.loop(1, top)
        def _(row):
            magnetic_row(run, row)
            electric_row(run, row, turn, state[run, 4, row - 1], state[run, 5, row - 1])

        magnetic_x(run, top)

    def boundary(run, turn):
        send_e(run, turn).wait_recv()
        state[run, 4, top] = partial[turn, run, 0] + c * jnp.where(
            is_last, 0.0, ghost_e[turn, run, 1]
        )
        state[run, 5, top] = partial[turn, run, 1] - c * jnp.where(
            is_last, 0.0, ghost_e[turn, run, 0]
        )
        electric_row(run, top, turn, state[run, 4, top - 1], state[run, 5, top - 1])
        if turn < STEPS - 1:
            make_partial(run, turn + 1)
            send_p(run, turn + 1).start()
        send_p(run, turn).wait_recv()
        prior_hy = jnp.where(is_first, 0.0, ghost_p[turn, run, 0] + c * state[run, 2, 0])
        prior_hz = jnp.where(is_first, 0.0, ghost_p[turn, run, 1] - c * state[run, 1, 0])
        send_e(run, turn).wait_send()
        electric_row(run, 0, turn, prior_hy, prior_hz)
        if turn < STEPS - 1:
            send_e(run, turn + 1).start()

    loads[0].wait()
    make_partial(0, 0)
    pl.semaphore_wait(barrier, 2)
    send_e(0, 0).start()
    send_p(0, 0).start()
    loads[1].wait()
    make_partial(1, 0)
    send_e(1, 0).start()
    send_p(1, 0).start()
    for copy in smalls:
        copy.wait()
    loads[2].wait()
    for run in range(2):
        level = lax.broadcasted_iota(jnp.int32, (NZ, NY), 0)
        hit = level == planes[run]
        sources[run] = jnp.where(hit, jnp.broadcast_to(profiles[run], (NZ, NY)), 0.0)

    interior(0, 0)
    interior(1, 0)
    for turn in range(STEPS):
        for run in range(2):
            boundary(run, turn)
            if turn < STEPS - 1:
                interior(run, turn + 1)

    outs = [
        pltpu.make_async_copy(state.at[0], forward_out.at[0], out_sem.at[0]),
        pltpu.make_async_copy(state.at[1], adjoint_out.at[0], out_sem.at[1]),
    ]
    for copy in outs:
        copy.start()
    local[...] = jnp.sum(acc[...], axis=1)
    last = pltpu.make_async_copy(local, local_out, out_sem.at[2])
    last.start()
    for turn in range(STEPS):
        for run in range(2):
            send_p(run, turn).wait_send()
    for copy in outs + [last]:
        copy.wait()


def yee(inverse, forward, adjoint, swave, sprofile, awave, aprofile, splane, mplane):
    rows = forward.shape[2]
    plane = (rows, NZ, NY)
    return pl.pallas_call(
        yee_kernel,
        out_shape=(
            jax.ShapeDtypeStruct(forward.shape, jnp.float32),
            jax.ShapeDtypeStruct(adjoint.shape, jnp.float32),
            jax.ShapeDtypeStruct((rows, NY), jnp.float32),
        ),
        in_specs=[pl.BlockSpec(memory_space=pl.ANY)] * 9,
        out_specs=[pl.BlockSpec(memory_space=pl.ANY)] * 3,
        scratch_shapes=[
            pltpu.VMEM((2, 6) + plane, jnp.float32),
            pltpu.VMEM(plane, jnp.float32),
            pltpu.VMEM((2, 1, STEPS), jnp.float32),
            pltpu.VMEM((2, 1, NY), jnp.float32),
            pltpu.VMEM((2, 1, 1), jnp.int32),
            pltpu.VMEM((2, NZ, NY), jnp.float32),
            pltpu.VMEM((STEPS, 2, 2, NZ, NY), jnp.float32),
            pltpu.VMEM((STEPS, 2, 2, NZ, NY), jnp.float32),
            pltpu.VMEM((STEPS, 2, 2, NZ, NY), jnp.float32),
            pltpu.VMEM((rows, 8, NY), jnp.float32),
            pltpu.VMEM((rows, NY), jnp.float32),
            pltpu.SemaphoreType.DMA((3,)),
            pltpu.SemaphoreType.DMA((6,)),
            pltpu.SemaphoreType.DMA((STEPS, 2)),
            pltpu.SemaphoreType.DMA((STEPS, 2)),
            pltpu.SemaphoreType.DMA((STEPS, 2)),
            pltpu.SemaphoreType.DMA((STEPS, 2)),
            pltpu.SemaphoreType.DMA((3,)),
        ],
        compiler_params=pltpu.CompilerParams(collective_id=0, has_side_effects=True),
        name="yee",
    )(inverse, forward, adjoint, swave, sprofile, awave, aprofile, splane, mplane)


def over_pieces(shard, axis):
    return lax.all_gather(shard, axis).sum(0)


def padded_2(cells, sides, width):
    for axis, dim in sides:
        count = lax.axis_size(axis)
        ends = count - 1
        head = lax.slice_in_dim(cells, 0, width, axis=dim)
        tail = lax.slice_in_dim(cells, cells.shape[dim] - width, cells.shape[dim], axis=dim)
        cells = jnp.concatenate(
            [
                lax.ppermute(tail, axis, [(i, (i + 1) % count) for i in range(ends)]),
                cells,
                lax.ppermute(head, axis, [((i + 1) % count, i) for i in range(ends)]),
            ],
            axis=dim,
        )
    return cells


def on_device(
    inverse_permittivity,
    forward_fields,
    adjoint_fields,
    source_wave,
    source_profile,
    adjoint_wave,
    adjoint_profile,
    source_plane,
    monitor_plane,
    radius_map,
    design_mask,
    design_density,
):
    forward_out, adjoint_out, local = yee(
        inverse_permittivity,
        forward_fields,
        adjoint_fields,
        source_wave,
        source_profile,
        adjoint_wave,
        adjoint_profile,
        source_plane.reshape(1, 1),
        monitor_plane.reshape(1, 1),
    )
    sent = over_pieces(local, "freq").T
    tiles = lax.all_to_all(sent, "slab", split_axis=0, concat_axis=1, tiled=True)
    tile_rows = tiles.shape[0]
    width = design_density.shape[1]
    columns = width // radius_map.shape[1]
    radius = jnp.repeat(radius_map, columns, axis=1).astype(jnp.float32)
    chosen = jnp.repeat(design_mask, columns, axis=1).astype(jnp.float32)
    scale = step_size / math.sqrt(3 * STEPS * NZ * FREQS)
    updated = design_density + scale * chosen * tiles
    rim = padded_2(updated, (("slab", 0),), RMAX)
    padded = jnp.pad(rim, ((0, 0), (RMAX, RMAX)))
    global_y = (
        lax.axis_index("slab") * tile_rows
        - RMAX
        + jnp.arange(tile_rows + 2 * RMAX, dtype=jnp.int32)
    )
    inside_y = ((global_y >= 0) & (global_y < NY)).astype(jnp.float32)
    inside_x = jnp.pad(jnp.ones((width,), jnp.float32), RMAX)
    inside = inside_y[:, None] * inside_x[None, :]
    numerator = jnp.zeros((tile_rows, width), jnp.float32)
    weight_total = jnp.zeros((tile_rows, width), jnp.float32)
    for offset_y in range(2 * RMAX + 1):
        for offset_x in range(2 * RMAX + 1):
            distance = jnp.sqrt(
                jnp.asarray((offset_y - RMAX) ** 2 + (offset_x - RMAX) ** 2, jnp.float32)
            )
            weight = jnp.maximum(radius - distance, 0.0)
            piece = padded[offset_y : offset_y + tile_rows, offset_x : offset_x + width]
            present = inside[offset_y : offset_y + tile_rows, offset_x : offset_x + width]
            numerator = numerator + weight * present * piece
            weight_total = weight_total + weight * present
    filtered = numerator / weight_total
    base = math.tanh(sharpness * midpoint)
    projected = (base + jnp.tanh(sharpness * (filtered - midpoint))) / (
        base + math.tanh(sharpness * (1.0 - midpoint))
    )
    return (forward_out, adjoint_out, projected)


def solution(mesh):
    return jax.shard_map(
        on_device,
        mesh=mesh,
        in_specs=(
            P("slab", None, None),
            P("freq", None, "slab", None, None),
            P("freq", None, "slab", None, None),
            P("freq", None),
            P("freq", None),
            P("freq", None),
            P("freq", None),
            P("freq"),
            P("freq"),
            P("slab", None),
            P("slab", None),
            P("slab", None),
        ),
        out_specs=(
            P("freq", None, "slab", None, None),
            P("freq", None, "slab", None, None),
            P("slab", None),
        ),
        check_vma=False,
    )
```

time: 146 us -> 78.7 us (0.54)
  the two profiles are of different devices: /device:TPU:6 before, /device:TPU:8 now
where the time goes in v1:
time: 78.7 us; the launch traced here: 78.4 us
  Pallas kernels  30.3 us (39%)
  starting transfers between devices  18.1 us (23%)
  waiting for transfers between devices  12 us (15%)
  local copies, waits for them, and re-layouts  7.49 us (10%)
  blocking collectives  6.95 us (9%)
  between operations  2.08 us (3%)
  other arithmetic  1.46 us (2%)
    pallas_call x1, Pallas kernels, yee(): pl.pallas_call(yee_kernel, out_shape=(jax.ShapeDtypeStruct(forward.shape,...  30.3 us
    all_to_all x1, waiting for transfers between devices, on_device(): lax.all_to_all(sent, 'slab', split_axis=0, concat_axis=1, tiled=True)  12 us
    all_to_all x1, starting transfers between devices, on_device(): lax.all_to_all(sent, 'slab', split_axis=0, concat_axis=1, tiled=True)  8 us
    ppermute x1, starting transfers between devices, padded_2(): lax.ppermute(head, axis, [((i + 1) % count, i) for i in range(ends)])  7.38 us
    all_gather x1, blocking collectives, over_pieces(): return lax.all_gather(shard, axis).sum(0)  6.95 us
    unnamed x12, local copies, waits for them, and re-layouts  3.94 us
    ppermute x1, starting transfers between devices, padded_2(): lax.ppermute(tail, axis, [(i, (i + 1) % count) for i in range(ends)])  2.68 us
  transfers between devices with their start and end apart: 3, of which 1 were waited for; matrix products, arithmetic and copies ran while one was open for 3% of the time, Pallas kernels for 0%

profile of v1, /device:TPU:8, one launch (start us, length us, event | category | flops | bytes accessed | tf_op | source)
XLA Modules:
  0.0 78.4 jit_solution(6521602183363144784)
XLA Ops:
  2.0 30.3 %yee.1 = (f32[1,6,8,24,512]{4,3,2,1,0:T(8,128)}, f32[1,6,8,24,512]{4,3,2,1,0:T(8,128)}, f32[8,512]{1,0:T(8,128)}) custom-call(f32[8,24,512]{2,1,0:T(8,128)} %inverse_hbm.1, f32[1,6,8,24,512]{4,3,2,1,0:T(8,128)} %forward_hbm.1, f32[1,6,8,24,512]{4,3,2,1,0:T(8,128)} %adjoint_hbm.1, f32[1,3]{1,0:T(1,128)} %swave_hbm.1, f32[1,512]{1,0:T(1,128)} %sprofile_hbm.1, ...), custom_call_target="tpu_custom_call" | custom-call | tf_op jit(solution)/shard_map/yee/pallas_call | solution.py:219
  32.3 7.0 %all-gather = f32[32,512]{1,0:T(8,128)S(1)} all-gather(f32[8,512]{1,0:T(8,128)} %get-tuple-element.8), channel_id=2, replica_groups=mesh['freq'=4,'slab'=64] {'freq'}, dimensions={0}, use_global_device_ids=true | all-gather | bytes 81920 | tf_op jit(solution)/shard_map/all_gather | solution.py:254
  39.3 0.2 all_to_all.14
  39.4 0.9 %copy.16 = f32[64,8,8]{1,2,0:T(8,128)} copy(f32[64,8,8]{1,0,2:T(8,128)S(1)} %all_to_all.14) | data formatting | bytes 32768 | tf_op jit(solution)/shard_map/all_to_all | solution.py:300
  40.3 8.0 %all-to-all-start = ((f32[64,8,8]{1,2,0:T(8,128)}), f32[64,8,8]{1,2,0:T(8,128)S(1)}, u32[]{:S(2)}, u32[]{:S(2)}) async-start(f32[64,8,8]{1,2,0:T(8,128)} %copy.16), calls=%async_computation | async-start | bytes 524288 | tf_op jit(solution)/shard_map/all_to_all | solution.py:300
  48.6 0.1 mul.395
  48.6 12.0 %all-to-all-done = f32[64,8,8]{1,2,0:T(8,128)S(1)} async-done(((f32[64,8,8]{1,2,0:T(8,128)}), f32[64,8,8]{1,2,0:T(8,128)S(1)}, u32[]{:S(2)}, u32[]{:S(2)}) %all-to-all-start) | async-done | bytes 16416 | tf_op jit(solution)/shard_map/all_to_all | solution.py:300
  60.6 0.1 copy.18
  60.8 2.7 %collective-permute-start = (f32[4,512]{1,0:T(4,128)S(1)}, f32[4,512]{1,0:T(4,128)S(1)}, u32[]{:S(2)}, u32[]{:S(2)}) collective-permute-start(f32[4,512]{1,0:T(4,128)S(1)} %get-tuple-element.9), channel_id=1, source_target_pairs={{0,1},{1,2},{2,3},{3,4},{4,5},{5,6},{6,7},{7,8},{8,9},{9,10},{10,1... | collective-permute-start | bytes 24584 | tf_op jit(solution)/shard_map/ppermute | solution.py:265
  63.4 7.4 %collective-permute-start.1 = (f32[4,512]{1,0:T(4,128)S(1)}, f32[4,512]{1,0:T(4,128)S(1)}, u32[]{:S(2)}, u32[]{:S(2)}) collective-permute-start(f32[4,512]{1,0:T(4,128)S(1)} %get-tuple-element.10), channel_id=1, source_target_pairs={{1,0},{2,1},{3,2},{4,3},{5,4},{6,5},{7,6},{8,7},{9,8},{10,9},{11,1... | collective-permute-start | bytes 24584 | tf_op jit(solution)/shard_map/ppermute | solution.py:267
  70.9 0.1 max.293
  71.1 0.1 max.296
  71.2 0.1 max.299
  71.4 0.1 max.302
  71.5 0.1 max.305
  71.7 0.1 max.308
  71.8 0.1 max.311
  72.0 0.1 max.314
  72.1 0.1 max.317
  73.1 0.1 select_maximum_fusion
  73.2 1.3 %add_multiply_fusion = f32[8,512]{1,0:T(8,128)} fusion(f32[16,520]{1,0:T(8,128)S(1)} %select_maximum_fusion, f32[16,520]{1,0:T(8,128)S(1)} %broadcast_multiply_fusion, f32[4,512]{1,0:T(4,128)S(1)} %collective-permute-done.1, f32[8,512]{1,0:T(8,128)S(1)} %multiply_add_fusion, f32[4,512]{1,0:T(4,128)S(1)} %collective-permute-done, f32[512]{0:T(512)S(1)} %max.335, ...), kind=kLoop, calls=%fused_computation.269 | loop fusion | flops 1372160 | bytes 2586624 | tf_op jit(solution)/shard_map/div | solution.py:332
  74.5 1.4 %copy.23 = f32[1,6,8,24,512]{4,3,2,1,0:T(8,128)} copy(f32[1,6,8,24,512]{4,3,2,1,0:T(8,128)S(1)} %copy-done.1) | data formatting | bytes 4718592
  75.9 1.1 %copy-done = f32[1,6,8,24,512]{4,3,2,1,0:T(8,128)S(1)} copy-done((f32[1,6,8,24,512]{4,3,2,1,0:T(8,128)S(1)}, f32[1,6,8,24,512]{4,3,2,1,0:T(8,128)}, u32[]{:S(2)}) %copy-start) | copy-done | bytes 2359320
  77.0 1.4 %copy.24 = f32[1,6,8,24,512]{4,3,2,1,0:T(8,128)} copy(f32[1,6,8,24,512]{4,3,2,1,0:T(8,128)S(1)} %copy-done) | data formatting | bytes 4718592
  (42 shorter events, 1.8 us)
Async XLA Ops:
  1.9 46.6 %copy-start.4 = (s32[1,8]{1,0:T(1,128)S(1)}, s32[1,8]{1,0:T(1,128)}, u32[]{:S(2)}) copy-start(s32[1,8]{1,0:T(1,128)} %param.22) | copy-start | bytes 100
  1.9 58.8 %copy-start.2 = (f32[8,512]{1,0:T(8,128)S(1)}, f32[8,512]{1,0:T(8,128)}, u32[]{:S(2)}) copy-start(f32[8,512]{1,0:T(8,128)} %param.23) | copy-start | bytes 49156
  1.9 68.9 %copy-start.3 = (s32[1,8]{1,0:T(1,128)S(1)}, s32[1,8]{1,0:T(1,128)}, u32[]{:S(2)}) copy-start(s32[1,8]{1,0:T(1,128)} %param.21) | copy-start | bytes 100
  39.2 35.2 %copy-start.1 = (f32[1,6,8,24,512]{4,3,2,1,0:T(8,128)S(1)}, f32[1,6,8,24,512]{4,3,2,1,0:T(8,128)}, u32[]{:S(2)}) copy-start(f32[1,6,8,24,512]{4,3,2,1,0:T(8,128)} %get-tuple-element.29) | copy-start | bytes 7077892
  40.3 20.4 %all-to-all-start = ((f32[64,8,8]{1,2,0:T(8,128)}), f32[64,8,8]{1,2,0:T(8,128)S(1)}, u32[]{:S(2)}, u32[]{:S(2)}) async-start(f32[64,8,8]{1,2,0:T(8,128)} %copy.16), calls=%async_computation | async-start | bytes 524288 | tf_op jit(solution)/shard_map/all_to_all | solution.py:300
  60.8 12.3 %collective-permute-start = (f32[4,512]{1,0:T(4,128)S(1)}, f32[4,512]{1,0:T(4,128)S(1)}, u32[]{:S(2)}, u32[]{:S(2)}) collective-permute-start(f32[4,512]{1,0:T(4,128)S(1)} %get-tuple-element.9), channel_id=1, source_target_pairs={{0,1},{1,2},{2,3},{3,4},{4,5},{5,6},{6,7},{7,8},{8,9},{9,10},{10,1... | collective-permute-start | bytes 24584 | tf_op jit(solution)/shard_map/ppermute | solution.py:265
  63.4 9.7 %collective-permute-start.1 = (f32[4,512]{1,0:T(4,128)S(1)}, f32[4,512]{1,0:T(4,128)S(1)}, u32[]{:S(2)}, u32[]{:S(2)}) collective-permute-start(f32[4,512]{1,0:T(4,128)S(1)} %get-tuple-element.10), channel_id=1, source_target_pairs={{1,0},{2,1},{3,2},{4,3},{5,4},{6,5},{7,6},{8,7},{9,8},{10,9},{11,1... | collective-permute-start | bytes 24584 | tf_op jit(solution)/shard_map/ppermute | solution.py:267
  74.5 2.5 %copy-start = (f32[1,6,8,24,512]{4,3,2,1,0:T(8,128)S(1)}, f32[1,6,8,24,512]{4,3,2,1,0:T(8,128)}, u32[]{:S(2)}) copy-start(f32[1,6,8,24,512]{4,3,2,1,0:T(8,128)} %get-tuple-element.30) | copy-start | bytes 7077892

commit v2 on v1

--- a/solution.py
+++ b/solution.py
@@ -42,9 +42,12 @@
 
 def yee_kernel(
     inverse_hbm, forward_hbm, adjoint_hbm, swave_hbm, sprofile_hbm, awave_hbm, aprofile_hbm, splane_hbm, mplane_hbm,
-    forward_out, adjoint_out, local_out,
-    state, inverse, waves, profiles, planes, sources, partial, ghost_e, ghost_p, acc, local,
+    radius_hbm, mask_hbm, density_hbm,
+    forward_out, adjoint_out, projected_out,
+    state, inverse, waves, profiles, planes, sources, partial, ghost_e, ghost_p, acc,
+    radius, mask, design, beside, weights, gathered, outgoing, incoming, projected,
     load_sem, small_sem, e_send, e_recv, p_send, p_recv, out_sem,
+    greet_sem, beside_send, beside_recv, freq_send, freq_recv, tile_send, tile_recv,
 ):
     count = lax.axis_size("slab")
     me = lax.axis_index("slab")
@@ -55,10 +58,19 @@
     top = rows - 1
     c = courant
 
+    group = lax.axis_index("freq")
+    groups = lax.axis_size("freq")
     barrier = pltpu.get_barrier_semaphore()
     for neighbour in (left, right):
         pl.semaphore_signal(
             barrier, inc=1, device_id={"slab": neighbour}, device_id_type=pl.DeviceIdType.MESH
+        )
+    for ahead in range(1, groups):
+        pl.semaphore_signal(
+            barrier,
+            inc=1,
+            device_id={"freq": lax.rem(group + ahead, groups)},
+            device_id_type=pl.DeviceIdType.MESH,
         )
 
     loads = [
@@ -73,6 +85,9 @@
         pltpu.make_async_copy(aprofile_hbm, profiles.at[1], small_sem.at[3]),
         pltpu.make_async_copy(splane_hbm, planes.at[0], small_sem.at[4]),
         pltpu.make_async_copy(mplane_hbm, planes.at[1], small_sem.at[5]),
+        pltpu.make_async_copy(radius_hbm, radius, small_sem.at[6]),
+        pltpu.make_async_copy(mask_hbm, mask, small_sem.at[7]),
+        pltpu.make_async_copy(density_hbm, design.at[0], small_sem.at[8]),
     ]
     for copy in loads + smalls:
         copy.start()
@@ -172,11 +187,63 @@
         if turn < STEPS - 1:
             send_e(run, turn + 1).start()
 
+    def greet(level):
+        for there in (me + count - (1 << level), me + (1 << level)):
+            pl.semaphore_signal(
+                greet_sem.at[level],
+                inc=1,
+                device_id={"slab": lax.rem(there, count)},
+                device_id_type=pl.DeviceIdType.MESH,
+            )
+
+    levels = 0
+    while (2 << levels) < count:
+        levels += 1
+
+    def greeted(level):
+        if level < levels:
+            pl.semaphore_wait(greet_sem.at[level], 2)
+            if level + 1 < levels:
+                greet(level + 1)
+
+    def send_beside(side):
+        return pltpu.make_async_remote_copy(
+            src_ref=design,
+            dst_ref=beside.at[side],
+            send_sem=beside_send.at[side],
+            recv_sem=beside_recv.at[side],
+            device_id={"slab": (right, left)[side]},
+            device_id_type=pl.DeviceIdType.MESH,
+        )
+
+    def send_freq(ahead):
+        return pltpu.make_async_remote_copy(
+            src_ref=gathered.at[group],
+            dst_ref=gathered.at[group],
+            send_sem=freq_send.at[ahead - 1],
+            recv_sem=freq_recv.at[ahead - 1],
+            device_id={"freq": lax.rem(group + ahead, groups)},
+            device_id_type=pl.DeviceIdType.MESH,
+        )
+
+    def send_tile(ahead):
+        there = lax.rem(me + ahead, count)
+        return pltpu.make_async_remote_copy(
+            src_ref=outgoing.at[there],
+            dst_ref=incoming.at[me],
+            send_sem=tile_send,
+            recv_sem=tile_recv,
+            device_id={"slab": there},
+            device_id_type=pl.DeviceIdType.MESH,
+        )
+
     loads[0].wait()
     make_partial(0, 0)
-    pl.semaphore_wait(barrier, 2)
+    pl.semaphore_wait(barrier, 2 + groups - 1)
     send_e(0, 0).start()
     send_p(0, 0).start()
+    if levels > 0:
+        greet(0)
     loads[1].wait()
     make_partial(1, 0)
     send_e(1, 0).start()
@@ -185,90 +252,222 @@
         copy.wait()
     loads[2].wait()
     for run in range(2):
-        level = lax.broadcasted_iota(jnp.int32, (NZ, NY), 0)
+        level = lax.broadcasted_iota(jnp.int32, sources.shape[1:], 0)
         hit = level == planes[run]
-        sources[run] = jnp.where(hit, jnp.broadcast_to(profiles[run], (NZ, NY)), 0.0)
+        sources[run] = jnp.where(hit, jnp.broadcast_to(profiles[run], hit.shape), 0.0)
+
+    width = density_hbm.shape[1]
+    scale = step_size / math.sqrt(3 * STEPS * NZ * FREQS)
+    tile_x = width // radius.shape[1]
+    column = lax.broadcasted_iota(jnp.int32, (8, width), 1)
+    line = lax.broadcasted_iota(jnp.int32, (8, width), 0)
+
+    def spread(table):
+        wide = jnp.zeros((8, width), jnp.float32)
+        for tile in range(table.shape[1]):
+            value = jnp.broadcast_to(table[:, tile : tile + 1], (8, width)).astype(jnp.float32)
+            wide = jnp.where(column // tile_x == tile, value, wide)
+        return wide
+
+    design[1] = scale * spread(mask)
+    reach = spread(radius)
+    rim_inside = ((line < 4) & (me < count - 1)) | ((line >= 4) & (me > 0))
+
+    def shift_x(v, by):
+        if by == 0:
+            return v
+        inside = (column + by >= 0) & (column + by < width)
+        return jnp.where(inside, pltpu.roll(v, (width - by) % width, 1), 0.0)
+
+    def shift_y(own, rim, by):
+        if by == 0:
+            return own
+        mixed = jnp.where(line < by, rim, own) if by > 0 else jnp.where(line >= 8 + by, rim, own)
+        return pltpu.roll(mixed, (8 - by) % 8, 0)
+
+    def rings(own, rim):
+        totals = {}
+        for up in range(RMAX + 1):
+            piece = shift_y(own, rim, up)
+            if up:
+                piece = piece + shift_y(own, rim, -up)
+            for over in range(RMAX + 1):
+                both = shift_x(piece, over)
+                if over:
+                    both = both + shift_x(piece, -over)
+                key = up * up + over * over
+                totals[key] = totals[key] + both if key in totals else both
+        return totals
+
+    def prepare_weights():
+        counts = rings(jnp.ones((8, width), jnp.float32), jnp.where(rim_inside, 1.0, 0.0))
+        total = jnp.zeros((8, width), jnp.float32)
+        for key in counts:
+            total = total + jnp.maximum(reach - math.sqrt(key), 0.0) * counts[key]
+        for place, key in enumerate(sorted(counts)):
+            weights[place] = jnp.maximum(reach - math.sqrt(key), 0.0) / total
 
     interior(0, 0)
+    greeted(0)
     interior(1, 0)
+    greeted(1)
     for turn in range(STEPS):
         for run in range(2):
             boundary(run, turn)
             if turn < STEPS - 1:
                 interior(run, turn + 1)
-
+            greeted(2 + 2 * turn + run)
+        if turn == STEPS - 2:
+            send_beside(0).start()
+            send_beside(1).start()
+            prepare_weights()
+
+    gathered[group] = jnp.sum(acc[...], axis=1)
+    for ahead in range(1, groups):
+        send_freq(ahead).start()
     outs = [
         pltpu.make_async_copy(state.at[0], forward_out.at[0], out_sem.at[0]),
         pltpu.make_async_copy(state.at[1], adjoint_out.at[0], out_sem.at[1]),
     ]
     for copy in outs:
         copy.start()
-    local[...] = jnp.sum(acc[...], axis=1)
-    last = pltpu.make_async_copy(local, local_out, out_sem.at[2])
+    for ahead in range(1, groups):
+        send_freq(ahead).wait_recv()
+    whole = gathered[0]
+    for index in range(1, groups):
+        whole = whole + gathered[index]
+
+    sub = lax.broadcasted_iota(jnp.int32, (8, 128), 0)
+    lane = lax.broadcasted_iota(jnp.int32, (8, 128), 1)
+
+    def swap_bits(v, sub_bit, lane_bit):
+        high, low = (sub >> sub_bit) & 1, (lane >> lane_bit) & 1
+        rows_by, lanes_by = 1 << sub_bit, 1 << lane_bit
+        from_high = pltpu.roll(pltpu.roll(v, 8 - rows_by, 0), lanes_by, 1)
+        from_low = pltpu.roll(pltpu.roll(v, rows_by, 0), 128 - lanes_by, 1)
+        return jnp.where(high == low, v, jnp.where(high == 0, from_high, from_low))
+
+    strips = []
+    for block in range(width // 128):
+        v = whole[:, 128 * block : 128 * (block + 1)]
+        for bit in range(3):
+            v = swap_bits(v, bit, bit)
+        for bit in range(3):
+            v = swap_bits(v, bit, 3 + bit)
+        strips += [v, pltpu.roll(v, 64, 1)]
+    pieces = len(strips)
+    for index in range(pieces):
+        mine, above, below = strips[index], strips[(index + 1) % pieces], strips[index - 1]
+        upper = pltpu.roll(jnp.where(sub == 0, above, mine), 7, 0)
+        lower = pltpu.roll(jnp.where(sub == 7, below, mine), 1, 0)
+        rim = jnp.where(lane < 32, upper, lower)
+        packed = jnp.where(lane < 64, mine, pltpu.roll(rim, 64, 1))
+        for row in range(8):
+            outgoing[8 * index + row] = packed[row : row + 1]
+    incoming[me] = outgoing[me]
+
+    @pl.loop(1, count)
+    def _(ahead):
+        send_tile(ahead).start()
+
+    for side in range(2):
+        send_beside(side).wait_recv()
+    rim_density = jnp.where(line < 4, beside[1, 0], beside[0, 0])
+    rim_scale = jnp.where(line < 4, beside[1, 1], beside[0, 1])
+    pltpu.make_async_copy(
+        incoming.at[pl.ds(0, count - 1)], incoming.at[pl.ds(0, count - 1)], tile_recv
+    ).wait()
+    own_parts, rim_parts = [], []
+    for index in range(0, pieces, 2):
+        halves = []
+        for half in (index, index + 1):
+            v = jnp.concatenate([incoming[8 * half + row] for row in range(8)], axis=0)
+            for bit in range(3):
+                v = swap_bits(v, bit, 3 + bit)
+            halves.append(v)
+        own_parts.append(jnp.where(lane < 64, halves[0], pltpu.roll(halves[1], 64, 1)))
+        rim_parts.append(jnp.where(lane < 64, pltpu.roll(halves[0], 64, 1), halves[1]))
+    own = design[0] + design[1] * jnp.concatenate(own_parts, axis=1)
+    rim = rim_density + rim_scale * jnp.concatenate(rim_parts, axis=1)
+    sums = rings(own, jnp.where(rim_inside, rim, 0.0))
+    filtered = jnp.zeros((8, width), jnp.float32)
+    for place, key in enumerate(sorted(sums)):
+        filtered = filtered + weights[place] * sums[key]
+    base = math.tanh(sharpness * midpoint)
+    projected[...] = (base + jnp.tanh(sharpness * (filtered - midpoint))) / (
+        base + math.tanh(sharpness * (1.0 - midpoint))
+    )
+    last = pltpu.make_async_copy(projected, projected_out, out_sem.at[2])
     last.start()
     for turn in range(STEPS):
         for run in range(2):
             send_p(run, turn).wait_send()
+    for side in range(2):
+        send_beside(side).wait_send()
+    for ahead in range(1, groups):
+        send_freq(ahead).wait_send()
+    pltpu.make_async_copy(
+        incoming.at[pl.ds(0, count - 1)], incoming.at[pl.ds(0, count - 1)], tile_send
+    ).wait()
     for copy in outs + [last]:
         copy.wait()
 
 
-def yee(inverse, forward, adjoint, swave, sprofile, awave, aprofile, splane, mplane):
-    rows = forward.shape[2]
-    plane = (rows, NZ, NY)
+def yee(*operands):
+    forward = operands[1]
+    density = operands[11]
+    rows, high, wide = forward.shape[2:]
+    plane = (rows, high, wide)
+    width = density.shape[1]
+    count = lax.axis_size("slab")
+    groups = lax.axis_size("freq")
     return pl.pallas_call(
         yee_kernel,
         out_shape=(
             jax.ShapeDtypeStruct(forward.shape, jnp.float32),
-            jax.ShapeDtypeStruct(adjoint.shape, jnp.float32),
-            jax.ShapeDtypeStruct((rows, NY), jnp.float32),
+            jax.ShapeDtypeStruct(forward.shape, jnp.float32),
+            jax.ShapeDtypeStruct(density.shape, jnp.float32),
         ),
-        in_specs=[pl.BlockSpec(memory_space=pl.ANY)] * 9,
+        in_specs=[pl.BlockSpec(memory_space=pl.ANY)] * 12,
         out_specs=[pl.BlockSpec(memory_space=pl.ANY)] * 3,
         scratch_shapes=[
             pltpu.VMEM((2, 6) + plane, jnp.float32),
             pltpu.VMEM(plane, jnp.float32),
             pltpu.VMEM((2, 1, STEPS), jnp.float32),
-            pltpu.VMEM((2, 1, NY), jnp.float32),
+            pltpu.VMEM((2, 1, wide), jnp.float32),
             pltpu.VMEM((2, 1, 1), jnp.int32),
-            pltpu.VMEM((2, NZ, NY), jnp.float32),
-            pltpu.VMEM((STEPS, 2, 2, NZ, NY), jnp.float32),
-            pltpu.VMEM((STEPS, 2, 2, NZ, NY), jnp.float32),
-            pltpu.VMEM((STEPS, 2, 2, NZ, NY), jnp.float32),
-            pltpu.VMEM((rows, 8, NY), jnp.float32),
-            pltpu.VMEM((rows, NY), jnp.float32),
+            pltpu.VMEM((2, high, wide), jnp.float32),
+            pltpu.VMEM((STEPS, 2, 2, high, wide), jnp.float32),
+            pltpu.VMEM((STEPS, 2, 2, high, wide), jnp.float32),
+            pltpu.VMEM((STEPS, 2, 2, high, wide), jnp.float32),
+            pltpu.VMEM((rows, 8, wide), jnp.float32),
+            pltpu.VMEM(operands[9].shape, jnp.int32),
+            pltpu.VMEM(operands[10].shape, jnp.int32),
+            pltpu.VMEM((2, 8, width), jnp.float32),
+            pltpu.VMEM((2, 2, 8, width), jnp.float32),
+            pltpu.VMEM((15, 8, width), jnp.float32),
+            pltpu.VMEM((groups, rows, wide), jnp.float32),
+            pltpu.VMEM((count, 1, 128), jnp.float32),
+            pltpu.VMEM((count, 1, 128), jnp.float32),
+            pltpu.VMEM((8, width), jnp.float32),
             pltpu.SemaphoreType.DMA((3,)),
-            pltpu.SemaphoreType.DMA((6,)),
+            pltpu.SemaphoreType.DMA((9,)),
             pltpu.SemaphoreType.DMA((STEPS, 2)),
             pltpu.SemaphoreType.DMA((STEPS, 2)),
             pltpu.SemaphoreType.DMA((STEPS, 2)),
             pltpu.SemaphoreType.DMA((STEPS, 2)),
             pltpu.SemaphoreType.DMA((3,)),
+            pltpu.SemaphoreType.REGULAR((8,)),
+            pltpu.SemaphoreType.DMA((2,)),
+            pltpu.SemaphoreType.DMA((2,)),
+            pltpu.SemaphoreType.DMA((3,)),
+            pltpu.SemaphoreType.DMA((3,)),
+            pltpu.SemaphoreType.DMA,
+            pltpu.SemaphoreType.DMA,
         ],
         compiler_params=pltpu.CompilerParams(collective_id=0, has_side_effects=True),
         name="yee",
-    )(inverse, forward, adjoint, swave, sprofile, awave, aprofile, splane, mplane)
-
-
-def over_pieces(shard, axis):
-    return lax.all_gather(shard, axis).sum(0)
-
-
-def padded_2(cells, sides, width):
-    for axis, dim in sides:
-        count = lax.axis_size(axis)
-        ends = count - 1
-        head = lax.slice_in_dim(cells, 0, width, axis=dim)
-        tail = lax.slice_in_dim(cells, cells.shape[dim] - width, cells.shape[dim], axis=dim)
-        cells = jnp.concatenate(
-            [
-                lax.ppermute(tail, axis, [(i, (i + 1) % count) for i in range(ends)]),
-                cells,
-                lax.ppermute(head, axis, [((i + 1) % count, i) for i in range(ends)]),
-            ],
-            axis=dim,
-        )
-    return cells
+    )(*operands)
 
 
 def on_device(
@@ -285,7 +484,7 @@
     design_mask,
     design_density,
 ):
-    forward_out, adjoint_out, local = yee(
+    return yee(
         inverse_permittivity,
         forward_fields,
         adjoint_fields,
@@ -295,44 +494,10 @@
         adjoint_profile,
         source_plane.reshape(1, 1),
         monitor_plane.reshape(1, 1),
+        radius_map,
+        design_mask,
+        design_density,
     )
-    sent = over_pieces(local, "freq").T
-    tiles = lax.all_to_all(sent, "slab", split_axis=0, concat_axis=1, tiled=True)
-    tile_rows = tiles.shape[0]
-    width = design_density.shape[1]
-    columns = width // radius_map.shape[1]
-    radius = jnp.repeat(radius_map, columns, axis=1).astype(jnp.float32)
-    chosen = jnp.repeat(design_mask, columns, axis=1).astype(jnp.float32)
-    scale = step_size / math.sqrt(3 * STEPS * NZ * FREQS)
-    updated = design_density + scale * chosen * tiles
-    rim = padded_2(updated, (("slab", 0),), RMAX)
-    padded = jnp.pad(rim, ((0, 0), (RMAX, RMAX)))
-    global_y = (
-        lax.axis_index("slab") * tile_rows
-        - RMAX
-        + jnp.arange(tile_rows + 2 * RMAX, dtype=jnp.int32)
-    )
-    inside_y = ((global_y >= 0) & (global_y < NY)).astype(jnp.float32)
-    inside_x = jnp.pad(jnp.ones((width,), jnp.float32), RMAX)
-    inside = inside_y[:, None] * inside_x[None, :]
-    numerator = jnp.zeros((tile_rows, width), jnp.float32)
-    weight_total = jnp.zeros((tile_rows, width), jnp.float32)
-    for offset_y in range(2 * RMAX + 1):
-        for offset_x in range(2 * RMAX + 1):
-            distance = jnp.sqrt(
-                jnp.asarray((offset_y - RMAX) ** 2 + (offset_x - RMAX) ** 2, jnp.float32)
-            )
-            weight = jnp.maximum(radius - distance, 0.0)
-            piece = padded[offset_y : offset_y + tile_rows, offset_x : offset_x + width]
-            present = inside[offset_y : offset_y + tile_rows, offset_x : offset_x + width]
-            numerator = numerator + weight * present * piece
-            weight_total = weight_total + weight * present
-    filtered = numerator / weight_total
-    base = math.tanh(sharpness * midpoint)
-    projected = (base + jnp.tanh(sharpness * (filtered - midpoint))) / (
-        base + math.tanh(sharpness * (1.0 - midpoint))
-    )
-    return (forward_out, adjoint_out, projected)
 
 
 def solution(mesh):

time: 78.7 us -> 49.8 us (0.63)
  the two profiles are of different devices: /device:TPU:8 before, /device:TPU:1 now
where the time goes in v2:
time: 49.8 us; the launch traced here: 49.7 us
  Pallas kernels  42.2 us (85%)
  local copies, waits for them, and re-layouts  5.57 us (11%)
  between operations  1.94 us (4%)
    pallas_call x1, Pallas kernels, yee(): pl.pallas_call(yee_kernel, out_shape=(jax.ShapeDtypeStruct(forward.shape,...  42.2 us
    unnamed x7, local copies, waits for them, and re-layouts  5.57 us

profile of v2, /device:TPU:1, one launch (start us, length us, event | category | flops | bytes accessed | tf_op | source)
XLA Modules:
  0.0 49.7 jit_solution(14001835551894473728)
XLA Ops:
  1.9 42.2 %yee.1 = (f32[1,6,8,24,512]{4,3,2,1,0:T(8,128)}, f32[1,6,8,24,512]{4,3,2,1,0:T(8,128)}, f32[8,512]{1,0:T(8,128)}) custom-call(f32[8,24,512]{2,1,0:T(8,128)} %inverse_hbm.1, f32[1,6,8,24,512]{4,3,2,1,0:T(8,128)} %forward_hbm.1, f32[1,6,8,24,512]{4,3,2,1,0:T(8,128)} %adjoint_hbm.1, f32[1,3]{1,0:T(1,128)} %swave_hbm.1, f32[1,512]{1,0:T(1,128)} %sprofile_hbm.1, ...), custom_call_target="tpu_custom_call" | custom-call | tf_op jit(solution)/shard_map/yee/pallas_call | solution.py:424
  44.1 0.0 copy-start
  44.1 3.5 %copy.20 = f32[1,6,8,24,512]{4,3,2,1,0:T(8,128)} copy(f32[1,6,8,24,512]{4,3,2,1,0:T(8,128)} %get-tuple-element.6) | data formatting | bytes 4718592
  47.7 0.0 copy-done
  47.7 0.0 copy-start.1
  47.7 1.4 %copy.21 = f32[1,6,8,24,512]{4,3,2,1,0:T(8,128)} copy(f32[1,6,8,24,512]{4,3,2,1,0:T(8,128)S(1)} %copy-done) | data formatting | bytes 4718592
  49.1 0.0 copy-done.1
  49.1 0.6 %copy.22 = f32[8,512]{1,0:T(8,128)} copy(f32[8,512]{1,0:T(8,128)S(1)} %copy-done.1) | data formatting | bytes 32768
Async XLA Ops:
  44.1 3.6 %copy-start = (f32[1,6,8,24,512]{4,3,2,1,0:T(8,128)S(1)}, f32[1,6,8,24,512]{4,3,2,1,0:T(8,128)}, u32[]{:S(2)}) copy-start(f32[1,6,8,24,512]{4,3,2,1,0:T(8,128)} %get-tuple-element.7) | copy-start | bytes 7077892
  47.7 1.4 %copy-start.1 = (f32[8,512]{1,0:T(8,128)S(1)}, f32[8,512]{1,0:T(8,128)}, u32[]{:S(2)}) copy-start(f32[8,512]{1,0:T(8,128)} %get-tuple-element.8) | copy-start | bytes 49156

commit v3 on v2

--- a/solution.py
+++ b/solution.py
@@ -12,6 +12,7 @@
 FREQS = 4
 STEPS = 3
 RMAX = 4
+SIDE_X, SIDE_Z, SIDE_Y = 4, 8, 2
 
 
 courant = 0.5
@@ -41,13 +42,13 @@
 
 
 def yee_kernel(
-    inverse_hbm, forward_hbm, adjoint_hbm, swave_hbm, sprofile_hbm, awave_hbm, aprofile_hbm, splane_hbm, mplane_hbm,
+    inverse_hbm, forward_hbm, adjoint_hbm, swave_hbm, sprofile_hbm, awave_hbm, aprofile_hbm, planes_hbm,
     radius_hbm, mask_hbm, density_hbm,
-    forward_out, adjoint_out, projected_out,
-    state, inverse, waves, profiles, planes, sources, partial, ghost_e, ghost_p, acc,
-    radius, mask, design, beside, weights, gathered, outgoing, incoming, projected,
-    load_sem, small_sem, e_send, e_recv, p_send, p_recv, out_sem,
-    greet_sem, beside_send, beside_recv, freq_send, freq_recv, tile_send, tile_recv,
+    state, projected,
+    inverse, waves, profiles, planes, sources, partial, ghost_e, ghost_p, acc,
+    radius, mask, design, beside, weights, outgoing, incoming,
+    load_sem, small_sem, e_send, e_recv, p_send, p_recv,
+    greet_sem, beside_send, beside_recv, tile_send, tile_recv,
 ):
     count = lax.axis_size("slab")
     me = lax.axis_index("slab")
@@ -60,41 +61,81 @@
 
     group = lax.axis_index("freq")
     groups = lax.axis_size("freq")
+    at_x, at_z, at_y = me % SIDE_X, (me // SIDE_X) % SIDE_Z, me // (SIDE_X * SIDE_Z)
+
+    def device(by_x=0, by_z=0, by_y=0, by_far=0, by_core=0):
+        far, core = (group // 2 + by_far) % 2, (group % 2 + by_core) % 2
+        slab = (
+            (at_y + by_y) % SIDE_Y * SIDE_Z + (at_z + by_z) % SIDE_Z
+        ) * SIDE_X + (at_x + by_x) % SIDE_X
+        return {"freq": far * 2 + core, "slab": slab}
+
+    line_x = [dict(by_x=by) for by in range(1, SIDE_X)]
+    line_y = [
+        dict(by_y=y, by_far=far, by_core=core)
+        for y in range(2)
+        for far in range(2)
+        for core in range(2)
+        if y + far + core
+    ]
+    near_z = [dict(by_z=1), dict(by_z=SIDE_Z - 1)]
+    next_z_two = [dict(by_z=2), dict(by_z=SIDE_Z - 2)]
+    rounds = [near_z, next_z_two, line_x, line_y]
+
+    def signal(semaphore, partners):
+        for partner in partners:
+            pl.semaphore_signal(
+                semaphore,
+                inc=1,
+                device_id=device(**partner),
+                device_id_type=pl.DeviceIdType.MESH,
+            )
+
     barrier = pltpu.get_barrier_semaphore()
     for neighbour in (left, right):
         pl.semaphore_signal(
             barrier, inc=1, device_id={"slab": neighbour}, device_id_type=pl.DeviceIdType.MESH
         )
-    for ahead in range(1, groups):
-        pl.semaphore_signal(
-            barrier,
-            inc=1,
-            device_id={"freq": lax.rem(group + ahead, groups)},
-            device_id_type=pl.DeviceIdType.MESH,
-        )
-
+    greetings = near_z + line_x + line_y
+    signal(barrier, greetings)
+
+    def greet(level):
+        signal(greet_sem.at[level], rounds[level])
+
+    def greeted(level):
+        if level < len(rounds):
+            pl.semaphore_wait(greet_sem.at[level], len(rounds[level]))
+            if level + 1 < len(rounds):
+                greet(level + 1)
+
+    fields = (forward_hbm, adjoint_hbm)
+    edges = [
+        pltpu.make_async_copy(fields[run].at[0, :, top], state.at[run, :, top], load_sem.at[run])
+        for run in range(2)
+    ]
     loads = [
-        pltpu.make_async_copy(forward_hbm.at[0], state.at[0], load_sem.at[0]),
-        pltpu.make_async_copy(adjoint_hbm.at[0], state.at[1], load_sem.at[1]),
-        pltpu.make_async_copy(inverse_hbm, inverse, load_sem.at[2]),
+        pltpu.make_async_copy(
+            fields[run].at[0, :, pl.ds(0, top)], state.at[run, :, pl.ds(0, top)], load_sem.at[2 + run]
+        )
+        for run in range(2)
     ]
+    medium = pltpu.make_async_copy(inverse_hbm, inverse, load_sem.at[4])
     smalls = [
         pltpu.make_async_copy(swave_hbm, waves.at[0], small_sem.at[0]),
         pltpu.make_async_copy(awave_hbm, waves.at[1], small_sem.at[1]),
         pltpu.make_async_copy(sprofile_hbm, profiles.at[0], small_sem.at[2]),
         pltpu.make_async_copy(aprofile_hbm, profiles.at[1], small_sem.at[3]),
-        pltpu.make_async_copy(splane_hbm, planes.at[0], small_sem.at[4]),
-        pltpu.make_async_copy(mplane_hbm, planes.at[1], small_sem.at[5]),
+        pltpu.make_async_copy(planes_hbm, planes, small_sem.at[4]),
         pltpu.make_async_copy(radius_hbm, radius, small_sem.at[6]),
         pltpu.make_async_copy(mask_hbm, mask, small_sem.at[7]),
         pltpu.make_async_copy(density_hbm, design.at[0], small_sem.at[8]),
     ]
-    for copy in loads + smalls:
+    for copy in edges + [loads[0], medium, loads[1]] + smalls:
         copy.start()
 
     def send_e(run, turn):
         return pltpu.make_async_remote_copy(
-            src_ref=state.at[run, pl.ds(1, 2), 0],
+            src_ref=state.at[run, pl.ds(1, 2), 0] if turn else fields[run].at[0, pl.ds(1, 2), 0],
             dst_ref=ghost_e.at[turn, run],
             send_sem=e_send.at[turn, run],
             recv_sem=e_recv.at[turn, run],
@@ -187,25 +228,6 @@
         if turn < STEPS - 1:
             send_e(run, turn + 1).start()
 
-    def greet(level):
-        for there in (me + count - (1 << level), me + (1 << level)):
-            pl.semaphore_signal(
-                greet_sem.at[level],
-                inc=1,
-                device_id={"slab": lax.rem(there, count)},
-                device_id_type=pl.DeviceIdType.MESH,
-            )
-
-    levels = 0
-    while (2 << levels) < count:
-        levels += 1
-
-    def greeted(level):
-        if level < levels:
-            pl.semaphore_wait(greet_sem.at[level], 2)
-            if level + 1 < levels:
-                greet(level + 1)
-
     def send_beside(side):
         return pltpu.make_async_remote_copy(
             src_ref=design,
@@ -216,41 +238,45 @@
             device_id_type=pl.DeviceIdType.MESH,
         )
 
-    def send_freq(ahead):
+    def send_tile(partner):
+        there = device(**partner)
         return pltpu.make_async_remote_copy(
-            src_ref=gathered.at[group],
-            dst_ref=gathered.at[group],
-            send_sem=freq_send.at[ahead - 1],
-            recv_sem=freq_recv.at[ahead - 1],
-            device_id={"freq": lax.rem(group + ahead, groups)},
-            device_id_type=pl.DeviceIdType.MESH,
-        )
-
-    def send_tile(ahead):
-        there = lax.rem(me + ahead, count)
-        return pltpu.make_async_remote_copy(
-            src_ref=outgoing.at[there],
-            dst_ref=incoming.at[me],
+            src_ref=outgoing.at[pl.ds(there["slab"], 1)],
+            dst_ref=incoming.at[pl.ds(group * count + me, 1)],
             send_sem=tile_send,
             recv_sem=tile_recv,
-            device_id={"slab": there},
+            device_id=there,
             device_id_type=pl.DeviceIdType.MESH,
         )
 
-    loads[0].wait()
+    def hops(partner):
+        side = min(partner["by_x"], SIDE_X - partner["by_x"])
+        return side + (1 if partner["by_y"] else 2 * partner["by_far"])
+
+    spokes = sorted(
+        (
+            dict(by_x=x, by_y=y, by_far=far, by_core=core)
+            for x in range(SIDE_X)
+            for y in range(SIDE_Y)
+            for far in range(2)
+            for core in range(2)
+        ),
+        key=hops,
+        reverse=True,
+    )
+
+    edges[0].wait()
     make_partial(0, 0)
-    pl.semaphore_wait(barrier, 2 + groups - 1)
+    pl.semaphore_wait(barrier, 2 + len(greetings))
     send_e(0, 0).start()
     send_p(0, 0).start()
-    if levels > 0:
-        greet(0)
-    loads[1].wait()
+    edges[1].wait()
     make_partial(1, 0)
     send_e(1, 0).start()
     send_p(1, 0).start()
+    greet(0)
     for copy in smalls:
         copy.wait()
-    loads[2].wait()
     for run in range(2):
         level = lax.broadcasted_iota(jnp.int32, sources.shape[1:], 0)
         hit = level == planes[run]
@@ -307,8 +333,11 @@
         for place, key in enumerate(sorted(counts)):
             weights[place] = jnp.maximum(reach - math.sqrt(key), 0.0) / total
 
+    medium.wait()
+    loads[0].wait()
     interior(0, 0)
     greeted(0)
+    loads[1].wait()
     interior(1, 0)
     greeted(1)
     for turn in range(STEPS):
@@ -322,20 +351,7 @@
             send_beside(1).start()
             prepare_weights()
 
-    gathered[group] = jnp.sum(acc[...], axis=1)
-    for ahead in range(1, groups):
-        send_freq(ahead).start()
-    outs = [
-        pltpu.make_async_copy(state.at[0], forward_out.at[0], out_sem.at[0]),
-        pltpu.make_async_copy(state.at[1], adjoint_out.at[0], out_sem.at[1]),
-    ]
-    for copy in outs:
-        copy.start()
-    for ahead in range(1, groups):
-        send_freq(ahead).wait_recv()
-    whole = gathered[0]
-    for index in range(1, groups):
-        whole = whole + gathered[index]
+    whole = jnp.sum(acc[...], axis=1)
 
     sub = lax.broadcasted_iota(jnp.int32, (8, 128), 0)
     lane = lax.broadcasted_iota(jnp.int32, (8, 128), 1)
@@ -362,26 +378,32 @@
         lower = pltpu.roll(jnp.where(sub == 7, below, mine), 1, 0)
         rim = jnp.where(lane < 32, upper, lower)
         packed = jnp.where(lane < 64, mine, pltpu.roll(rim, 64, 1))
-        for row in range(8):
-            outgoing[8 * index + row] = packed[row : row + 1]
-    incoming[me] = outgoing[me]
-
-    @pl.loop(1, count)
-    def _(ahead):
-        send_tile(ahead).start()
+        outgoing[8 * index : 8 * index + 8] = packed
+
+    @pl.loop(0, SIDE_Z - 1)
+    def _(order):
+        by_z = SIDE_Z // 2 + order % 2 * -(order + 1) // 2 + (order + 1) % 2 * order // 2
+        for spoke in spokes:
+            send_tile(dict(by_z=by_z, **spoke)).start()
+
+    for spoke in spokes:
+        if any(spoke.values()):
+            send_tile(spoke).start()
+    incoming[pl.ds(group * count + me, 1)] = outgoing[pl.ds(me, 1)]
 
     for side in range(2):
         send_beside(side).wait_recv()
     rim_density = jnp.where(line < 4, beside[1, 0], beside[0, 0])
     rim_scale = jnp.where(line < 4, beside[1, 1], beside[0, 1])
-    pltpu.make_async_copy(
-        incoming.at[pl.ds(0, count - 1)], incoming.at[pl.ds(0, count - 1)], tile_recv
-    ).wait()
+    everyone = incoming.at[pl.ds(0, groups * count - 1)]
+    pltpu.make_async_copy(everyone, everyone, tile_recv).wait()
     own_parts, rim_parts = [], []
     for index in range(0, pieces, 2):
         halves = []
         for half in (index, index + 1):
-            v = jnp.concatenate([incoming[8 * half + row] for row in range(8)], axis=0)
+            v = incoming[8 * half : 8 * half + 8]
+            for other in range(1, groups):
+                v = v + incoming[other * count + 8 * half : other * count + 8 * half + 8]
             for bit in range(3):
                 v = swap_bits(v, bit, 3 + bit)
             halves.append(v)
@@ -397,77 +419,96 @@
     projected[...] = (base + jnp.tanh(sharpness * (filtered - midpoint))) / (
         base + math.tanh(sharpness * (1.0 - midpoint))
     )
-    last = pltpu.make_async_copy(projected, projected_out, out_sem.at[2])
-    last.start()
     for turn in range(STEPS):
         for run in range(2):
             send_p(run, turn).wait_send()
     for side in range(2):
         send_beside(side).wait_send()
-    for ahead in range(1, groups):
-        send_freq(ahead).wait_send()
-    pltpu.make_async_copy(
-        incoming.at[pl.ds(0, count - 1)], incoming.at[pl.ds(0, count - 1)], tile_send
-    ).wait()
-    for copy in outs + [last]:
+    pltpu.make_async_copy(everyone, everyone, tile_send).wait()
+
+
+def write_kernel(state, projected, forward_out, adjoint_out, projected_out, sems):
+    copies = [
+        pltpu.make_async_copy(state.at[run, comp], out.at[0, comp], sems.at[6 * run + comp])
+        for run, out in enumerate((forward_out, adjoint_out))
+        for comp in range(6)
+    ]
+    copies.append(pltpu.make_async_copy(projected, projected_out, sems.at[12]))
+    for copy in copies:
+        copy.start()
+    for copy in copies:
         copy.wait()
 
 
 def yee(*operands):
     forward = operands[1]
-    density = operands[11]
+    density = operands[10]
     rows, high, wide = forward.shape[2:]
     plane = (rows, high, wide)
     width = density.shape[1]
     count = lax.axis_size("slab")
     groups = lax.axis_size("freq")
+    operands = [
+        operand if place == 7 else pltpu.with_memory_space_constraint(operand, pltpu.HBM)
+        for place, operand in enumerate(operands)
+    ]
+    state, projected = pl.pallas_call(
+        yee_kernel,
+        out_shape=(
+            pltpu.VMEM((2, 6) + plane, jnp.float32),
+            pltpu.VMEM(density.shape, jnp.float32),
+        ),
+        in_specs=[pl.BlockSpec(memory_space=pl.ANY)] * 11,
+        out_specs=[pl.BlockSpec(memory_space=pltpu.VMEM)] * 2,
+        scratch_shapes=[
+            pltpu.VMEM(plane, jnp.float32),
+            pltpu.VMEM((2, 1, STEPS), jnp.float32),
+            pltpu.VMEM((2, 1, wide), jnp.float32),
+            pltpu.SMEM((2,), jnp.int32),
+            pltpu.VMEM((2, high, wide), jnp.float32),
+            pltpu.VMEM((STEPS, 2, 2, high, wide), jnp.float32),
+            pltpu.VMEM((STEPS, 2, 2, high, wide), jnp.float32),
+            pltpu.VMEM((STEPS, 2, 2, high, wide), jnp.float32),
+            pltpu.VMEM((rows, 8, wide), jnp.float32),
+            pltpu.VMEM(operands[8].shape, jnp.int32),
+            pltpu.VMEM(operands[9].shape, jnp.int32),
+            pltpu.VMEM((2, 8, width), jnp.float32),
+            pltpu.VMEM((2, 2, 8, width), jnp.float32),
+            pltpu.VMEM((15, 8, width), jnp.float32),
+            pltpu.VMEM((count, 128), jnp.float32),
+            pltpu.VMEM((groups * count, 128), jnp.float32),
+            pltpu.SemaphoreType.DMA((5,)),
+            pltpu.SemaphoreType.DMA((9,)),
+            pltpu.SemaphoreType.DMA((STEPS, 2)),
+            pltpu.SemaphoreType.DMA((STEPS, 2)),
+            pltpu.SemaphoreType.DMA((STEPS, 2)),
+            pltpu.SemaphoreType.DMA((STEPS, 2)),
+            pltpu.SemaphoreType.REGULAR((4,)),
+            pltpu.SemaphoreType.DMA((2,)),
+            pltpu.SemaphoreType.DMA((2,)),
+            pltpu.SemaphoreType.DMA,
+            pltpu.SemaphoreType.DMA,
+        ],
+        compiler_params=pltpu.CompilerParams(
+            collective_id=0, has_side_effects=True, vmem_limit_bytes=40 << 20
+        ),
+        name="yee",
+    )(*operands)
+    state = pltpu.with_memory_space_constraint(state, pltpu.VMEM)
+    projected = pltpu.with_memory_space_constraint(projected, pltpu.VMEM)
     return pl.pallas_call(
-        yee_kernel,
+        write_kernel,
         out_shape=(
             jax.ShapeDtypeStruct(forward.shape, jnp.float32),
             jax.ShapeDtypeStruct(forward.shape, jnp.float32),
             jax.ShapeDtypeStruct(density.shape, jnp.float32),
         ),
-        in_specs=[pl.BlockSpec(memory_space=pl.ANY)] * 12,
+        in_specs=[pl.BlockSpec(memory_space=pltpu.VMEM)] * 2,
         out_specs=[pl.BlockSpec(memory_space=pl.ANY)] * 3,
-        scratch_shapes=[
-            pltpu.VMEM((2, 6) + plane, jnp.float32),
-            pltpu.VMEM(plane, jnp.float32),
-            pltpu.VMEM((2, 1, STEPS), jnp.float32),
-            pltpu.VMEM((2, 1, wide), jnp.float32),
-            pltpu.VMEM((2, 1, 1), jnp.int32),
-            pltpu.VMEM((2, high, wide), jnp.float32),
-            pltpu.VMEM((STEPS, 2, 2, high, wide), jnp.float32),
-            pltpu.VMEM((STEPS, 2, 2, high, wide), jnp.float32),
-            pltpu.VMEM((STEPS, 2, 2, high, wide), jnp.float32),
-            pltpu.VMEM((rows, 8, wide), jnp.float32),
-            pltpu.VMEM(operands[9].shape, jnp.int32),
-            pltpu.VMEM(operands[10].shape, jnp.int32),
-            pltpu.VMEM((2, 8, width), jnp.float32),
-            pltpu.VMEM((2, 2, 8, width), jnp.float32),
-            pltpu.VMEM((15, 8, width), jnp.float32),
-            pltpu.VMEM((groups, rows, wide), jnp.float32),
-            pltpu.VMEM((count, 1, 128), jnp.float32),
-            pltpu.VMEM((count, 1, 128), jnp.float32),
-            pltpu.VMEM((8, width), jnp.float32),
-            pltpu.SemaphoreType.DMA((3,)),
-            pltpu.SemaphoreType.DMA((9,)),
-            pltpu.SemaphoreType.DMA((STEPS, 2)),
-            pltpu.SemaphoreType.DMA((STEPS, 2)),
-            pltpu.SemaphoreType.DMA((STEPS, 2)),
-            pltpu.SemaphoreType.DMA((STEPS, 2)),
-            pltpu.SemaphoreType.DMA((3,)),
-            pltpu.SemaphoreType.REGULAR((8,)),
-            pltpu.SemaphoreType.DMA((2,)),
-            pltpu.SemaphoreType.DMA((2,)),
-            pltpu.SemaphoreType.DMA((3,)),
-            pltpu.SemaphoreType.DMA((3,)),
-            pltpu.SemaphoreType.DMA,
-            pltpu.SemaphoreType.DMA,
-        ],
-        compiler_params=pltpu.CompilerParams(collective_id=0, has_side_effects=True),
-        name="yee",
-    )(*operands)
+        scratch_shapes=[pltpu.SemaphoreType.DMA((13,))],
+        compiler_params=pltpu.CompilerParams(vmem_limit_bytes=8 << 20),
+        name="write",
+    )(state, projected)
 
 
 def on_device(
@@ -492,8 +533,7 @@
         source_profile,
         adjoint_wave,
         adjoint_profile,
-        source_plane.reshape(1, 1),
-        monitor_plane.reshape(1, 1),
+        jnp.concatenate([source_plane, monitor_plane]),
         radius_map,
         design_mask,
         design_density,

time: 49.8 us -> 45.7 us (0.918)
  local copies, waits for them, and re-layouts: 5.57 us -> 0 us
  Pallas kernels: 42.2 us -> 43.6 us
    unnamed x7 -> x0, local copies, waits for them, and re-layouts: 5.57 us -> none
    pallas_call x1 -> x2, Pallas kernels: 42.2 us -> 43.6 us  [the longest x1 41.3 us: yee(): pl.pallas_call(yee_kernel, out_shape=(pltpu.VMEM((2, 6) + plane, jnp.floa...]
where the time goes in v3:
time: 45.7 us; the launch traced here: 45.6 us
  Pallas kernels  43.6 us (95%)
  between operations  1.93 us (4%)
    pallas_call x1, Pallas kernels, yee(): pl.pallas_call(yee_kernel, out_shape=(pltpu.VMEM((2, 6) + plane, jnp.floa...  41.3 us
    pallas_call x1, Pallas kernels, yee(): pl.pallas_call(write_kernel, out_shape=(jax.ShapeDtypeStruct(forward.shap...  2.29 us

profile of v3, /device:TPU:1, one launch (start us, length us, event | category | flops | bytes accessed | tf_op | source)
XLA Modules:
  0.0 45.6 jit_solution(10018829137356802568)
XLA Ops:
  1.9 0.1 pad_add_fusion.planes_hbm
  2.0 41.3 %yee.1 = (f32[2,6,8,24,512]{4,3,2,1,0:T(8,128)S(1)}, f32[8,512]{1,0:T(8,128)S(1)}) custom-call(f32[8,24,512]{2,1,0:T(8,128)} %inverse_hbm.1, f32[1,6,8,24,512]{4,3,2,1,0:T(8,128)} %forward_hbm.1, f32[1,6,8,24,512]{4,3,2,1,0:T(8,128)} %adjoint_hbm.1, f32[1,3]{1,0:T(1,128)} %swave_hbm.1, f32[1,512]{1,0:T(1,128)} %sprofile_hbm.1, f32[1,3]{1,0:T(1,128)} %awave_hbm.1, ...), custom_call_target="tpu_custom_call" | custom-call | tf_op jit(solution)/shard_map/yee/pallas_call | solution.py:455
  43.3 2.3 %write.1 = (f32[1,6,8,24,512]{4,3,2,1,0:T(8,128)}, f32[1,6,8,24,512]{4,3,2,1,0:T(8,128)}, f32[8,512]{1,0:T(8,128)}) custom-call(f32[2,6,8,24,512]{4,3,2,1,0:T(8,128)S(1)} %get-tuple-element.5.state, f32[8,512]{1,0:T(8,128)S(1)} %get-tuple-element.6.projected), custom_call_target="tpu_custom_call" | custom-call | tf_op jit(solution)/shard_map/write/pallas_call | solution.py:499

commit v4 on v3

--- a/solution.py
+++ b/solution.py
@@ -41,14 +41,56 @@
     return jnp.where(row == 0, 0.0, pltpu.roll(v, 1, 0))
 
 
+def swap_bits(v, sub_bit, lane_bit):
+    sub = lax.broadcasted_iota(jnp.int32, (8, 128), 0)
+    lane = lax.broadcasted_iota(jnp.int32, (8, 128), 1)
+    high, low = (sub >> sub_bit) & 1, (lane >> lane_bit) & 1
+    rows_by, lanes_by = 1 << sub_bit, 1 << lane_bit
+    from_high = pltpu.roll(pltpu.roll(v, 8 - rows_by, 0), lanes_by, 1)
+    from_low = pltpu.roll(pltpu.roll(v, rows_by, 0), 128 - lanes_by, 1)
+    return jnp.where(high == low, v, jnp.where(high == 0, from_high, from_low))
+
+
+def shift_x(v, by):
+    if by == 0:
+        return v
+    width = v.shape[1]
+    column = lax.broadcasted_iota(jnp.int32, v.shape, 1)
+    inside = (column + by >= 0) & (column + by < width)
+    return jnp.where(inside, pltpu.roll(v, (width - by) % width, 1), 0.0)
+
+
+def shift_y(own, rim, by):
+    if by == 0:
+        return own
+    line = lax.broadcasted_iota(jnp.int32, own.shape, 0)
+    mixed = jnp.where(line < by, rim, own) if by > 0 else jnp.where(line >= 8 + by, rim, own)
+    return pltpu.roll(mixed, (8 - by) % 8, 0)
+
+
+def rings(own, rim):
+    totals = {}
+    for up in range(RMAX + 1):
+        piece = shift_y(own, rim, up)
+        if up:
+            piece = piece + shift_y(own, rim, -up)
+        for over in range(RMAX + 1):
+            both = shift_x(piece, over)
+            if over:
+                both = both + shift_x(piece, -over)
+            key = up * up + over * over
+            totals[key] = totals[key] + both if key in totals else both
+    return totals
+
+
 def yee_kernel(
     inverse_hbm, forward_hbm, adjoint_hbm, swave_hbm, sprofile_hbm, awave_hbm, aprofile_hbm, planes_hbm,
     radius_hbm, mask_hbm, density_hbm,
-    state, projected,
+    state, incoming, swapped, finish, weights,
     inverse, waves, profiles, planes, sources, partial, ghost_e, ghost_p, acc,
-    radius, mask, design, beside, weights, outgoing, incoming,
+    radius, mask, beside, pairs, local, late, outgoing,
     load_sem, small_sem, e_send, e_recv, p_send, p_recv,
-    greet_sem, beside_send, beside_recv, tile_send, tile_recv,
+    greet_sem, beside_send, beside_recv, pair_send, pair_recv, tile_send, tile_recv, cross_send, cross_recv,
 ):
     count = lax.axis_size("slab")
     me = lax.axis_index("slab")
@@ -61,14 +103,17 @@
 
     group = lax.axis_index("freq")
     groups = lax.axis_size("freq")
-    at_x, at_z, at_y = me % SIDE_X, (me // SIDE_X) % SIDE_Z, me // (SIDE_X * SIDE_Z)
+    at_x, at_line = lax.rem(me, SIDE_X), lax.div(me, SIDE_X)
+    at_z, at_y = lax.rem(at_line, SIDE_Z), lax.div(at_line, SIDE_Z)
+    at_far, at_core = lax.div(group, 2), lax.rem(group, 2)
+
+    def turned(at, by, side):
+        return lax.rem(at + by, side) if by else at
 
     def device(by_x=0, by_z=0, by_y=0, by_far=0, by_core=0):
-        far, core = (group // 2 + by_far) % 2, (group % 2 + by_core) % 2
-        slab = (
-            (at_y + by_y) % SIDE_Y * SIDE_Z + (at_z + by_z) % SIDE_Z
-        ) * SIDE_X + (at_x + by_x) % SIDE_X
-        return {"freq": far * 2 + core, "slab": slab}
+        far, core = turned(at_far, by_far, 2), turned(at_core, by_core, 2)
+        line = turned(at_y, by_y, SIDE_Y) * SIDE_Z + turned(at_z, by_z, SIDE_Z)
+        return {"freq": far * 2 + core, "slab": line * SIDE_X + turned(at_x, by_x, SIDE_X)}
 
     line_x = [dict(by_x=by) for by in range(1, SIDE_X)]
     line_y = [
@@ -91,14 +136,6 @@
                 device_id_type=pl.DeviceIdType.MESH,
             )
 
-    barrier = pltpu.get_barrier_semaphore()
-    for neighbour in (left, right):
-        pl.semaphore_signal(
-            barrier, inc=1, device_id={"slab": neighbour}, device_id_type=pl.DeviceIdType.MESH
-        )
-    greetings = near_z + line_x + line_y
-    signal(barrier, greetings)
-
     def greet(level):
         signal(greet_sem.at[level], rounds[level])
 
@@ -128,9 +165,18 @@
         pltpu.make_async_copy(planes_hbm, planes, small_sem.at[4]),
         pltpu.make_async_copy(radius_hbm, radius, small_sem.at[6]),
         pltpu.make_async_copy(mask_hbm, mask, small_sem.at[7]),
-        pltpu.make_async_copy(density_hbm, design.at[0], small_sem.at[8]),
+        pltpu.make_async_copy(density_hbm, finish.at[0], small_sem.at[8]),
     ]
-    for copy in edges + [loads[0], medium, loads[1]] + smalls:
+    for copy in edges:
+        copy.start()
+    barrier = pltpu.get_barrier_semaphore()
+    for neighbour in (left, right):
+        pl.semaphore_signal(
+            barrier, inc=1, device_id={"slab": neighbour}, device_id_type=pl.DeviceIdType.MESH
+        )
+    greetings = line_y + line_x + near_z
+    signal(barrier, greetings)
+    for copy in [loads[0], medium, loads[1]] + smalls:
         copy.start()
 
     def send_e(run, turn):
@@ -193,7 +239,9 @@
                 elec_x * state[0, 0, row] + elec_y * state[0, 1, row] + elec_z * state[0, 2, row]
             )
             folded = total[0:8] + total[8:16] + total[16:24]
-            if turn == 0:
+            if turn == STEPS - 1 and isinstance(row, int):
+                late[row // top] = jnp.sum(folded, axis=0)
+            elif turn == 0:
                 acc[row] = folded
             else:
                 acc[row] = acc[row] + folded
@@ -230,7 +278,7 @@
 
     def send_beside(side):
         return pltpu.make_async_remote_copy(
-            src_ref=design,
+            src_ref=finish.at[pl.ds(0, 2)],
             dst_ref=beside.at[side],
             send_sem=beside_send.at[side],
             recv_sem=beside_recv.at[side],
@@ -238,32 +286,46 @@
             device_id_type=pl.DeviceIdType.MESH,
         )
 
-    def send_tile(partner):
-        there = device(**partner)
+    crossed = at_core * 2 + at_far
+
+    def send_tile(partner, sends, receives):
+        there = device(**partner)["slab"]
         return pltpu.make_async_remote_copy(
-            src_ref=outgoing.at[pl.ds(there["slab"], 1)],
-            dst_ref=incoming.at[pl.ds(group * count + me, 1)],
-            send_sem=tile_send,
-            recv_sem=tile_recv,
-            device_id=there,
+            src_ref=outgoing.at[pl.ds(there, 1)],
+            dst_ref=incoming.at[pl.ds(me, 1)],
+            send_sem=sends,
+            recv_sem=receives,
+            device_id={"freq": crossed, "slab": there},
             device_id_type=pl.DeviceIdType.MESH,
         )
 
-    def hops(partner):
-        side = min(partner["by_x"], SIDE_X - partner["by_x"])
-        return side + (1 if partner["by_y"] else 2 * partner["by_far"])
+    def hops(by):
+        far_x, far_z = min(by["by_x"], SIDE_X - by["by_x"]), min(by["by_z"], SIDE_Z - by["by_z"])
+        return far_x + far_z + by["by_y"]
 
     spokes = sorted(
         (
-            dict(by_x=x, by_y=y, by_far=far, by_core=core)
+            dict(by_x=x, by_z=z, by_y=y)
             for x in range(SIDE_X)
+            for z in range(SIDE_Z)
             for y in range(SIDE_Y)
-            for far in range(2)
-            for core in range(2)
+            if x + z + y
         ),
         key=hops,
         reverse=True,
     )
+
+    def swap_cores(source, target, place):
+        return pltpu.make_async_remote_copy(
+            src_ref=source,
+            dst_ref=target,
+            send_sem=pair_send.at[place],
+            recv_sem=pair_recv.at[place],
+            device_id=device(by_core=1),
+            device_id_type=pl.DeviceIdType.MESH,
+        )
+
+    pair = swap_cores(pairs.at[at_core], pairs.at[at_core], 0)
 
     edges[0].wait()
     make_partial(0, 0)
@@ -295,35 +357,9 @@
             wide = jnp.where(column // tile_x == tile, value, wide)
         return wide
 
-    design[1] = scale * spread(mask)
+    finish[1] = scale * spread(mask)
     reach = spread(radius)
     rim_inside = ((line < 4) & (me < count - 1)) | ((line >= 4) & (me > 0))
-
-    def shift_x(v, by):
-        if by == 0:
-            return v
-        inside = (column + by >= 0) & (column + by < width)
-        return jnp.where(inside, pltpu.roll(v, (width - by) % width, 1), 0.0)
-
-    def shift_y(own, rim, by):
-        if by == 0:
-            return own
-        mixed = jnp.where(line < by, rim, own) if by > 0 else jnp.where(line >= 8 + by, rim, own)
-        return pltpu.roll(mixed, (8 - by) % 8, 0)
-
-    def rings(own, rim):
-        totals = {}
-        for up in range(RMAX + 1):
-            piece = shift_y(own, rim, up)
-            if up:
-                piece = piece + shift_y(own, rim, -up)
-            for over in range(RMAX + 1):
-                both = shift_x(piece, over)
-                if over:
-                    both = both + shift_x(piece, -over)
-                key = up * up + over * over
-                totals[key] = totals[key] + both if key in totals else both
-        return totals
 
     def prepare_weights():
         counts = rings(jnp.ones((8, width), jnp.float32), jnp.where(rim_inside, 1.0, 0.0))
@@ -350,19 +386,21 @@
             send_beside(0).start()
             send_beside(1).start()
             prepare_weights()
-
-    whole = jnp.sum(acc[...], axis=1)
-
+            local[...] = jnp.sum(acc[...], axis=1)
+
+    ends = late[...]
+    whole = local[...] + jnp.where(line == 0, ends[0:1], 0.0)
+    pairs[at_core] = whole + jnp.where(line == top, ends[1:2], 0.0)
+    pair.start()
+    for side in range(2):
+        send_beside(side).wait_recv()
+    for place in range(2):
+        rim = jnp.where(line < 4, beside[1, place], beside[0, place])
+        finish[2 + place] = jnp.where(rim_inside, rim, 0.0)
+    pair.wait_recv()
+    whole = pairs[0] + pairs[1]
     sub = lax.broadcasted_iota(jnp.int32, (8, 128), 0)
     lane = lax.broadcasted_iota(jnp.int32, (8, 128), 1)
-
-    def swap_bits(v, sub_bit, lane_bit):
-        high, low = (sub >> sub_bit) & 1, (lane >> lane_bit) & 1
-        rows_by, lanes_by = 1 << sub_bit, 1 << lane_bit
-        from_high = pltpu.roll(pltpu.roll(v, 8 - rows_by, 0), lanes_by, 1)
-        from_low = pltpu.roll(pltpu.roll(v, rows_by, 0), 128 - lanes_by, 1)
-        return jnp.where(high == low, v, jnp.where(high == 0, from_high, from_low))
-
     strips = []
     for block in range(width // 128):
         v = whole[:, 128 * block : 128 * (block + 1)]
@@ -380,62 +418,70 @@
         packed = jnp.where(lane < 64, mine, pltpu.roll(rim, 64, 1))
         outgoing[8 * index : 8 * index + 8] = packed
 
-    @pl.loop(0, SIDE_Z - 1)
-    def _(order):
-        by_z = SIDE_Z // 2 + order % 2 * -(order + 1) // 2 + (order + 1) % 2 * order // 2
-        for spoke in spokes:
-            send_tile(dict(by_z=by_z, **spoke)).start()
-
     for spoke in spokes:
-        if any(spoke.values()):
-            send_tile(spoke).start()
-    incoming[pl.ds(group * count + me, 1)] = outgoing[pl.ds(me, 1)]
-
-    for side in range(2):
-        send_beside(side).wait_recv()
-    rim_density = jnp.where(line < 4, beside[1, 0], beside[0, 0])
-    rim_scale = jnp.where(line < 4, beside[1, 1], beside[0, 1])
-    everyone = incoming.at[pl.ds(0, groups * count - 1)]
+        send_tile(spoke, tile_send, tile_recv).start()
+
+    @pl.when(at_far == at_core)
+    def _():
+        incoming[pl.ds(me, 1)] = outgoing[pl.ds(me, 1)]
+
+    @pl.when(at_far != at_core)
+    def _():
+        cross = send_tile({}, cross_send, cross_recv)
+        cross.start()
+        cross.wait()
+
+    everyone = incoming.at[pl.ds(0, len(spokes))]
     pltpu.make_async_copy(everyone, everyone, tile_recv).wait()
-    own_parts, rim_parts = [], []
-    for index in range(0, pieces, 2):
-        halves = []
-        for half in (index, index + 1):
-            v = incoming[8 * half : 8 * half + 8]
-            for other in range(1, groups):
-                v = v + incoming[other * count + 8 * half : other * count + 8 * half + 8]
-            for bit in range(3):
-                v = swap_bits(v, bit, 3 + bit)
-            halves.append(v)
-        own_parts.append(jnp.where(lane < 64, halves[0], pltpu.roll(halves[1], 64, 1)))
-        rim_parts.append(jnp.where(lane < 64, pltpu.roll(halves[0], 64, 1), halves[1]))
-    own = design[0] + design[1] * jnp.concatenate(own_parts, axis=1)
-    rim = rim_density + rim_scale * jnp.concatenate(rim_parts, axis=1)
-    sums = rings(own, jnp.where(rim_inside, rim, 0.0))
-    filtered = jnp.zeros((8, width), jnp.float32)
-    for place, key in enumerate(sorted(sums)):
-        filtered = filtered + weights[place] * sums[key]
-    base = math.tanh(sharpness * midpoint)
-    projected[...] = (base + jnp.tanh(sharpness * (filtered - midpoint))) / (
-        base + math.tanh(sharpness * (1.0 - midpoint))
-    )
+    swap = swap_cores(incoming, swapped, 1)
+    swap.start()
     for turn in range(STEPS):
         for run in range(2):
             send_p(run, turn).wait_send()
     for side in range(2):
         send_beside(side).wait_send()
+    pair.wait_send()
     pltpu.make_async_copy(everyone, everyone, tile_send).wait()
-
-
-def write_kernel(state, projected, forward_out, adjoint_out, projected_out, sems):
+    swap.wait()
+
+
+def write_kernel(
+    state, incoming, swapped, finish, weights, forward_out, adjoint_out, projected_out, projected, sems
+):
     copies = [
         pltpu.make_async_copy(state.at[run, comp], out.at[0, comp], sems.at[6 * run + comp])
         for run, out in enumerate((forward_out, adjoint_out))
         for comp in range(6)
     ]
-    copies.append(pltpu.make_async_copy(projected, projected_out, sems.at[12]))
     for copy in copies:
         copy.start()
+
+    @pl.when(lax.axis_index("slab") >= 0)
+    def _():
+        lane = lax.broadcasted_iota(jnp.int32, (8, 128), 1)
+        own_parts, rim_parts = [], []
+        for index in range(0, incoming.shape[0] // 8, 2):
+            halves = []
+            for half in (index, index + 1):
+                v = incoming[8 * half : 8 * half + 8] + swapped[8 * half : 8 * half + 8]
+                for bit in range(3):
+                    v = swap_bits(v, bit, 3 + bit)
+                halves.append(v)
+            own_parts.append(jnp.where(lane < 64, halves[0], pltpu.roll(halves[1], 64, 1)))
+            rim_parts.append(jnp.where(lane < 64, pltpu.roll(halves[0], 64, 1), halves[1]))
+        own = finish[0] + finish[1] * jnp.concatenate(own_parts, axis=1)
+        rim = finish[2] + finish[3] * jnp.concatenate(rim_parts, axis=1)
+        sums = rings(own, rim)
+        filtered = jnp.zeros_like(own)
+        for place, key in enumerate(sorted(sums)):
+            filtered = filtered + weights[place] * sums[key]
+        base = math.tanh(sharpness * midpoint)
+        projected[...] = (base + jnp.tanh(sharpness * (filtered - midpoint))) / (
+            base + math.tanh(sharpness * (1.0 - midpoint))
+        )
+
+    copies.append(pltpu.make_async_copy(projected, projected_out, sems.at[12]))
+    copies[-1].start()
     for copy in copies:
         copy.wait()
 
@@ -452,14 +498,17 @@
         operand if place == 7 else pltpu.with_memory_space_constraint(operand, pltpu.HBM)
         for place, operand in enumerate(operands)
     ]
-    state, projected = pl.pallas_call(
+    results = pl.pallas_call(
         yee_kernel,
         out_shape=(
             pltpu.VMEM((2, 6) + plane, jnp.float32),
-            pltpu.VMEM(density.shape, jnp.float32),
+            pltpu.VMEM((count, 128), jnp.float32),
+            pltpu.VMEM((count, 128), jnp.float32),
+            pltpu.VMEM((4, 8, width), jnp.float32),
+            pltpu.VMEM((15, 8, width), jnp.float32),
         ),
         in_specs=[pl.BlockSpec(memory_space=pl.ANY)] * 11,
-        out_specs=[pl.BlockSpec(memory_space=pltpu.VMEM)] * 2,
+        out_specs=[pl.BlockSpec(memory_space=pltpu.VMEM)] * 5,
         scratch_shapes=[
             pltpu.VMEM(plane, jnp.float32),
             pltpu.VMEM((2, 1, STEPS), jnp.float32),
@@ -472,11 +521,11 @@
             pltpu.VMEM((rows, 8, wide), jnp.float32),
             pltpu.VMEM(operands[8].shape, jnp.int32),
             pltpu.VMEM(operands[9].shape, jnp.int32),
-            pltpu.VMEM((2, 8, width), jnp.float32),
             pltpu.VMEM((2, 2, 8, width), jnp.float32),
-            pltpu.VMEM((15, 8, width), jnp.float32),
+            pltpu.VMEM((2, rows, wide), jnp.float32),
+            pltpu.VMEM((rows, wide), jnp.float32),
+            pltpu.VMEM((2, wide), jnp.float32),
             pltpu.VMEM((count, 128), jnp.float32),
-            pltpu.VMEM((groups * count, 128), jnp.float32),
             pltpu.SemaphoreType.DMA((5,)),
             pltpu.SemaphoreType.DMA((9,)),
             pltpu.SemaphoreType.DMA((STEPS, 2)),
@@ -486,6 +535,10 @@
             pltpu.SemaphoreType.REGULAR((4,)),
             pltpu.SemaphoreType.DMA((2,)),
             pltpu.SemaphoreType.DMA((2,)),
+            pltpu.SemaphoreType.DMA((2,)),
+            pltpu.SemaphoreType.DMA((2,)),
+            pltpu.SemaphoreType.DMA,
+            pltpu.SemaphoreType.DMA,
             pltpu.SemaphoreType.DMA,
             pltpu.SemaphoreType.DMA,
         ],
@@ -494,8 +547,7 @@
         ),
         name="yee",
     )(*operands)
-    state = pltpu.with_memory_space_constraint(state, pltpu.VMEM)
-    projected = pltpu.with_memory_space_constraint(projected, pltpu.VMEM)
+    results = [pltpu.with_memory_space_constraint(result, pltpu.VMEM) for result in results]
     return pl.pallas_call(
         write_kernel,
         out_shape=(
@@ -503,12 +555,12 @@
             jax.ShapeDtypeStruct(forward.shape, jnp.float32),
             jax.ShapeDtypeStruct(density.shape, jnp.float32),
         ),
-        in_specs=[pl.BlockSpec(memory_space=pltpu.VMEM)] * 2,
+        in_specs=[pl.BlockSpec(memory_space=pltpu.VMEM)] * 5,
         out_specs=[pl.BlockSpec(memory_space=pl.ANY)] * 3,
-        scratch_shapes=[pltpu.SemaphoreType.DMA((13,))],
+        scratch_shapes=[pltpu.VMEM(density.shape, jnp.float32), pltpu.SemaphoreType.DMA((13,))],
         compiler_params=pltpu.CompilerParams(vmem_limit_bytes=8 << 20),
         name="write",
-    )(state, projected)
+    )(*results)
 
 
 def on_device(

time: 45.7 us -> 44.5 us (0.974)
  Pallas kernels: 43.6 us -> 42.4 us
    pallas_call x1, Pallas kernels: 41.3 us -> 40.1 us  [yee(): pl.pallas_call(yee_kernel, out_shape=(pltpu.VMEM((2, 6) + plane, jnp.floa...]
where the time goes in v4:
time: 44.5 us; the launch traced here: 44.4 us
  Pallas kernels  42.4 us (95%)
  between operations  1.93 us (4%)
    pallas_call x1, Pallas kernels, yee(): pl.pallas_call(yee_kernel, out_shape=(pltpu.VMEM((2, 6) + plane, jnp.floa...  40.1 us
    pallas_call x1, Pallas kernels, yee(): pl.pallas_call(write_kernel, out_shape=(jax.ShapeDtypeStruct(forward.shap...  2.29 us

profile of v4, /device:TPU:1, one launch (start us, length us, event | category | flops | bytes accessed | tf_op | source)
XLA Modules:
  0.0 44.4 jit_solution(9483118854992347775)
XLA Ops:
  1.9 0.1 pad_add_fusion.planes_hbm
  2.0 40.1 %yee.1 = (f32[2,6,8,24,512]{4,3,2,1,0:T(8,128)S(1)}, f32[64,128]{1,0:T(8,128)S(1)}, f32[64,128]{1,0:T(8,128)S(1)}, f32[4,8,512]{2,1,0:T(8,128)S(1)}, f32[15,8,512]{2,1,0:T(8,128)S(1)}) custom-call(f32[8,24,512]{2,1,0:T(8,128)} %inverse_hbm.1, f32[1,6,8,24,512]{4,3,2,1,0:T(8,128)} %forward_hbm.1, f32[1,6,8,24,512]{4,3,2,1,0:T(8,128)} %adjoint_hbm.1, ...), custom_call_target="tpu_custom_call" | custom-call | tf_op jit(solution)/shard_map/yee/pallas_call | solution.py:501
  42.1 2.3 %write.1 = (f32[1,6,8,24,512]{4,3,2,1,0:T(8,128)}, f32[1,6,8,24,512]{4,3,2,1,0:T(8,128)}, f32[8,512]{1,0:T(8,128)}) custom-call(f32[2,6,8,24,512]{4,3,2,1,0:T(8,128)S(1)} %get-tuple-element.8.state, f32[64,128]{1,0:T(8,128)S(1)} %get-tuple-element.9.incoming, f32[64,128]{1,0:T(8,128)S(1)} %get-tuple-element.10.swapped, ...), custom_call_target="tpu_custom_call" | custom-call | tf_op jit(solution)/shard_map/write/pallas_call | solution.py:551

commit v5 on v4

--- a/solution.py
+++ b/solution.py
@@ -86,11 +86,11 @@
 def yee_kernel(
     inverse_hbm, forward_hbm, adjoint_hbm, swave_hbm, sprofile_hbm, awave_hbm, aprofile_hbm, planes_hbm,
     radius_hbm, mask_hbm, density_hbm,
-    state, incoming, swapped, finish, weights,
-    inverse, waves, profiles, planes, sources, partial, ghost_e, ghost_p, acc,
+    state, incoming, finish, weights,
+    inverse, waves, profiles, planes, sources, partial, ghost_e, ghost_p, edge, soon, acc,
     radius, mask, beside, pairs, local, late, outgoing,
     load_sem, small_sem, e_send, e_recv, p_send, p_recv,
-    greet_sem, beside_send, beside_recv, pair_send, pair_recv, tile_send, tile_recv, cross_send, cross_recv,
+    greet_sem, beside_send, beside_recv, pair_send, pair_recv, tile_send, tile_recv,
 ):
     count = lax.axis_size("slab")
     me = lax.axis_index("slab")
@@ -181,7 +181,7 @@
 
     def send_e(run, turn):
         return pltpu.make_async_remote_copy(
-            src_ref=state.at[run, pl.ds(1, 2), 0] if turn else fields[run].at[0, pl.ds(1, 2), 0],
+            src_ref=edge.at[turn - 1, run] if turn else fields[run].at[0, pl.ds(1, 2), 0],
             dst_ref=ghost_e.at[turn, run],
             send_sem=e_send.at[turn, run],
             recv_sem=e_recv.at[turn, run],
@@ -220,6 +220,16 @@
             state[run, 1, row + 1] - elec_y - (next_y(elec_x) - elec_x)
         )
 
+    def keep(row, turn, elec_x, elec_y, elec_z):
+        total = elec_x * state[0, 0, row] + elec_y * state[0, 1, row] + elec_z * state[0, 2, row]
+        folded = total[0:8] + total[8:16] + total[16:24]
+        if turn == STEPS - 1 and isinstance(row, int):
+            late[row // top] = jnp.sum(folded, axis=0)
+        elif turn == 0:
+            acc[row] = folded
+        else:
+            acc[row] = acc[row] + folded
+
     def electric_row(run, row, turn, prior_hy, prior_hz):
         magn_x, magn_y, magn_z = (state[run, comp, row] for comp in range(3, 6))
         scaled = c * inverse[row]
@@ -235,16 +245,7 @@
         state[run, 1, row] = elec_y
         state[run, 2, row] = elec_z
         if run == 1:
-            total = (
-                elec_x * state[0, 0, row] + elec_y * state[0, 1, row] + elec_z * state[0, 2, row]
-            )
-            folded = total[0:8] + total[8:16] + total[16:24]
-            if turn == STEPS - 1 and isinstance(row, int):
-                late[row // top] = jnp.sum(folded, axis=0)
-            elif turn == 0:
-                acc[row] = folded
-            else:
-                acc[row] = acc[row] + folded
+            keep(row, turn, elec_x, elec_y, elec_z)
 
     def interior(run, turn):
         magnetic_row(run, 0)
@@ -255,26 +256,72 @@
             electric_row(run, row, turn, state[run, 4, row - 1], state[run, 5, row - 1])
 
         magnetic_x(run, top)
+        ready(run, turn)
+
+    def ready(run, turn):
+        magn_x, magn_y, magn_z = (state[run, comp, 0] for comp in range(3, 6))
+        scaled = c * inverse[0]
+        reached = jnp.where(is_first, 0.0, scaled)
+        source = sources[run] * waves[run, :, turn : turn + 1]
+        elec_y, elec_z = state[run, 1, 0], state[run, 2, 0]
+        soon[run, 5] = (
+            state[run, 0, 0]
+            + scaled * (magn_z - prior_y(magn_z) - (magn_y - prior_z(magn_y)))
+            + source
+        )
+        soon[run, 0] = (
+            elec_y + scaled * (magn_x - prior_z(magn_x) - magn_z) - reached * (c * elec_y)
+        )
+        soon[run, 1] = (
+            elec_z + scaled * (magn_y - (magn_x - prior_y(magn_x))) - reached * (c * elec_z)
+        )
+        magn_x = state[run, 3, top]
+        scaled = c * inverse[top]
+        soon[run, 2] = state[run, 0, top] + source
+        soon[run, 3] = state[run, 1, top] + scaled * (
+            magn_x - prior_z(magn_x) + state[run, 5, top - 1]
+        )
+        soon[run, 4] = state[run, 2, top] - scaled * (
+            magn_x - prior_y(magn_x) + state[run, 4, top - 1]
+        )
 
     def boundary(run, turn):
+        send_p(run, turn).wait_recv()
+        reached = jnp.where(is_first, 0.0, c * inverse[0])
+        elec_y = soon[run, 0] + reached * ghost_p[turn, run, 1]
+        elec_z = soon[run, 1] - reached * ghost_p[turn, run, 0]
+        if turn < STEPS - 1:
+            edge[turn, run, 0] = elec_y
+            edge[turn, run, 1] = elec_z
+            send_e(run, turn + 1).start()
+        else:
+            state[run, 1, 0] = elec_y
+            state[run, 2, 0] = elec_z
         send_e(run, turn).wait_recv()
-        state[run, 4, top] = partial[turn, run, 0] + c * jnp.where(
-            is_last, 0.0, ghost_e[turn, run, 1]
-        )
-        state[run, 5, top] = partial[turn, run, 1] - c * jnp.where(
-            is_last, 0.0, ghost_e[turn, run, 0]
-        )
-        electric_row(run, top, turn, state[run, 4, top - 1], state[run, 5, top - 1])
+        state[run, 0, 0] = soon[run, 5]
         if turn < STEPS - 1:
-            make_partial(run, turn + 1)
+            state[run, 1, 0] = elec_y
+            state[run, 2, 0] = elec_z
+        scaled = c * inverse[top]
+        magn_y = partial[turn, run, 0] + c * jnp.where(is_last, 0.0, ghost_e[turn, run, 1])
+        magn_z = partial[turn, run, 1] - c * jnp.where(is_last, 0.0, ghost_e[turn, run, 0])
+        elec_x = soon[run, 2] + scaled * (
+            magn_z - prior_y(magn_z) - (magn_y - prior_z(magn_y))
+        )
+        elec_y = soon[run, 3] - scaled * magn_z
+        elec_z = soon[run, 4] + scaled * magn_y
+        if turn < STEPS - 1:
+            partial[turn + 1, run, 0] = magn_y - c * (next_z(elec_x) - elec_x + elec_z)
+            partial[turn + 1, run, 1] = magn_z + c * (elec_y + next_y(elec_x) - elec_x)
             send_p(run, turn + 1).start()
-        send_p(run, turn).wait_recv()
-        prior_hy = jnp.where(is_first, 0.0, ghost_p[turn, run, 0] + c * state[run, 2, 0])
-        prior_hz = jnp.where(is_first, 0.0, ghost_p[turn, run, 1] - c * state[run, 1, 0])
-        send_e(run, turn).wait_send()
-        electric_row(run, 0, turn, prior_hy, prior_hz)
-        if turn < STEPS - 1:
-            send_e(run, turn + 1).start()
+        state[run, 4, top] = magn_y
+        state[run, 5, top] = magn_z
+        state[run, 0, top] = elec_x
+        state[run, 1, top] = elec_y
+        state[run, 2, top] = elec_z
+        if run == 1:
+            for row in (0, top):
+                keep(row, turn, *(state[1, comp, row] for comp in range(3)))
 
     def send_beside(side):
         return pltpu.make_async_remote_copy(
@@ -286,46 +333,45 @@
             device_id_type=pl.DeviceIdType.MESH,
         )
 
-    crossed = at_core * 2 + at_far
-
-    def send_tile(partner, sends, receives):
-        there = device(**partner)["slab"]
+    def send_tile(partner):
+        there = device(**partner)
         return pltpu.make_async_remote_copy(
-            src_ref=outgoing.at[pl.ds(there, 1)],
-            dst_ref=incoming.at[pl.ds(me, 1)],
-            send_sem=sends,
-            recv_sem=receives,
-            device_id={"freq": crossed, "slab": there},
+            src_ref=outgoing.at[pl.ds(there["slab"], 1)],
+            dst_ref=incoming.at[pl.ds(at_far * count + me, 1)],
+            send_sem=tile_send,
+            recv_sem=tile_recv,
+            device_id=there,
             device_id_type=pl.DeviceIdType.MESH,
         )
 
     def hops(by):
         far_x, far_z = min(by["by_x"], SIDE_X - by["by_x"]), min(by["by_z"], SIDE_Z - by["by_z"])
-        return far_x + far_z + by["by_y"]
+        return far_x + far_z + (1 if by["by_y"] else 2 * by["by_far"])
 
     spokes = sorted(
         (
-            dict(by_x=x, by_z=z, by_y=y)
+            dict(by_x=x, by_z=z, by_y=y, by_far=far)
             for x in range(SIDE_X)
             for z in range(SIDE_Z)
             for y in range(SIDE_Y)
-            if x + z + y
+            for far in range(2)
+            if x + z + y + far
         ),
         key=hops,
         reverse=True,
     )
 
-    def swap_cores(source, target, place):
+    def swap_cores(source, target):
         return pltpu.make_async_remote_copy(
             src_ref=source,
             dst_ref=target,
-            send_sem=pair_send.at[place],
-            recv_sem=pair_recv.at[place],
+            send_sem=pair_send,
+            recv_sem=pair_recv,
             device_id=device(by_core=1),
             device_id_type=pl.DeviceIdType.MESH,
         )
 
-    pair = swap_cores(pairs.at[at_core], pairs.at[at_core], 0)
+    pair = swap_cores(pairs.at[at_core], pairs.at[at_core])
 
     edges[0].wait()
     make_partial(0, 0)
@@ -419,34 +465,22 @@
         outgoing[8 * index : 8 * index + 8] = packed
 
     for spoke in spokes:
-        send_tile(spoke, tile_send, tile_recv).start()
-
-    @pl.when(at_far == at_core)
-    def _():
-        incoming[pl.ds(me, 1)] = outgoing[pl.ds(me, 1)]
-
-    @pl.when(at_far != at_core)
-    def _():
-        cross = send_tile({}, cross_send, cross_recv)
-        cross.start()
-        cross.wait()
-
+        send_tile(spoke).start()
+    incoming[pl.ds(at_far * count + me, 1)] = outgoing[pl.ds(me, 1)]
     everyone = incoming.at[pl.ds(0, len(spokes))]
     pltpu.make_async_copy(everyone, everyone, tile_recv).wait()
-    swap = swap_cores(incoming, swapped, 1)
-    swap.start()
     for turn in range(STEPS):
         for run in range(2):
+            send_e(run, turn).wait_send()
             send_p(run, turn).wait_send()
     for side in range(2):
         send_beside(side).wait_send()
     pair.wait_send()
     pltpu.make_async_copy(everyone, everyone, tile_send).wait()
-    swap.wait()
 
 
 def write_kernel(
-    state, incoming, swapped, finish, weights, forward_out, adjoint_out, projected_out, projected, sems
+    state, incoming, finish, weights, forward_out, adjoint_out, projected_out, projected, sems
 ):
     copies = [
         pltpu.make_async_copy(state.at[run, comp], out.at[0, comp], sems.at[6 * run + comp])
@@ -460,10 +494,11 @@
     def _():
         lane = lax.broadcasted_iota(jnp.int32, (8, 128), 1)
         own_parts, rim_parts = [], []
-        for index in range(0, incoming.shape[0] // 8, 2):
+        count = incoming.shape[0] // 2
+        for index in range(0, count // 8, 2):
             halves = []
             for half in (index, index + 1):
-                v = incoming[8 * half : 8 * half + 8] + swapped[8 * half : 8 * half + 8]
+                v = incoming[8 * half : 8 * half + 8] + incoming[count + 8 * half : count + 8 * half + 8]
                 for bit in range(3):
                     v = swap_bits(v, bit, 3 + bit)
                 halves.append(v)
@@ -502,13 +537,12 @@
         yee_kernel,
         out_shape=(
             pltpu.VMEM((2, 6) + plane, jnp.float32),
-            pltpu.VMEM((count, 128), jnp.float32),
-            pltpu.VMEM((count, 128), jnp.float32),
+            pltpu.VMEM((2 * count, 128), jnp.float32),
             pltpu.VMEM((4, 8, width), jnp.float32),
             pltpu.VMEM((15, 8, width), jnp.float32),
         ),
         in_specs=[pl.BlockSpec(memory_space=pl.ANY)] * 11,
-        out_specs=[pl.BlockSpec(memory_space=pltpu.VMEM)] * 5,
+        out_specs=[pl.BlockSpec(memory_space=pltpu.VMEM)] * 4,
         scratch_shapes=[
             pltpu.VMEM(plane, jnp.float32),
             pltpu.VMEM((2, 1, STEPS), jnp.float32),
@@ -518,6 +552,8 @@
             pltpu.VMEM((STEPS, 2, 2, high, wide), jnp.float32),
             pltpu.VMEM((STEPS, 2, 2, high, wide), jnp.float32),
             pltpu.VMEM((STEPS, 2, 2, high, wide), jnp.float32),
+            pltpu.VMEM((STEPS - 1, 2, 2, high, wide), jnp.float32),
+            pltpu.VMEM((2, 6, high, wide), jnp.float32),
             pltpu.VMEM((rows, 8, wide), jnp.float32),
             pltpu.VMEM(operands[8].shape, jnp.int32),
             pltpu.VMEM(operands[9].shape, jnp.int32),
@@ -533,8 +569,6 @@
             pltpu.SemaphoreType.DMA((STEPS, 2)),
             pltpu.SemaphoreType.DMA((STEPS, 2)),
             pltpu.SemaphoreType.REGULAR((4,)),
-            pltpu.SemaphoreType.DMA((2,)),
-            pltpu.SemaphoreType.DMA((2,)),
             pltpu.SemaphoreType.DMA((2,)),
             pltpu.SemaphoreType.DMA((2,)),
             pltpu.SemaphoreType.DMA,
@@ -555,7 +589,7 @@
             jax.ShapeDtypeStruct(forward.shape, jnp.float32),
             jax.ShapeDtypeStruct(density.shape, jnp.float32),
         ),
-        in_specs=[pl.BlockSpec(memory_space=pltpu.VMEM)] * 5,
+        in_specs=[pl.BlockSpec(memory_space=pltpu.VMEM)] * 4,
         out_specs=[pl.BlockSpec(memory_space=pl.ANY)] * 3,
         scratch_shapes=[pltpu.VMEM(density.shape, jnp.float32), pltpu.SemaphoreType.DMA((13,))],
         compiler_params=pltpu.CompilerParams(vmem_limit_bytes=8 << 20),

time: 44.5 us -> 43.5 us (0.978)
  Pallas kernels: 42.4 us -> 41.4 us
    pallas_call x1, Pallas kernels: 40.1 us -> 39.1 us  [yee(): pl.pallas_call(yee_kernel, out_shape=(pltpu.VMEM((2, 6) + plane, jnp.floa...]
where the time goes in v5:
time: 43.5 us; the launch traced here: 43.4 us
  Pallas kernels  41.4 us (95%)
  between operations  1.93 us (4%)
    pallas_call x1, Pallas kernels, yee(): pl.pallas_call(yee_kernel, out_shape=(pltpu.VMEM((2, 6) + plane, jnp.floa...  39.1 us
    pallas_call x1, Pallas kernels, yee(): pl.pallas_call(write_kernel, out_shape=(jax.ShapeDtypeStruct(forward.shap...  2.29 us

profile of v5, /device:TPU:1, one launch (start us, length us, event | category | flops | bytes accessed | tf_op | source)
XLA Modules:
  0.0 43.4 jit_solution(8794004903275687113)
XLA Ops:
  1.9 0.1 pad_add_fusion.planes_hbm
  2.0 39.1 %yee.1 = (f32[2,6,8,24,512]{4,3,2,1,0:T(8,128)S(1)}, f32[128,128]{1,0:T(8,128)S(1)}, f32[4,8,512]{2,1,0:T(8,128)S(1)}, f32[15,8,512]{2,1,0:T(8,128)S(1)}) custom-call(f32[8,24,512]{2,1,0:T(8,128)} %inverse_hbm.1, f32[1,6,8,24,512]{4,3,2,1,0:T(8,128)} %forward_hbm.1, f32[1,6,8,24,512]{4,3,2,1,0:T(8,128)} %adjoint_hbm.1, f32[1,3]{1,0:T(1,128)} %swave_hbm.1, ...), custom_call_target="tpu_custom_call" | custom-call | tf_op jit(solution)/shard_map/yee/pallas_call | solution.py:536
  41.1 2.3 %write.1 = (f32[1,6,8,24,512]{4,3,2,1,0:T(8,128)}, f32[1,6,8,24,512]{4,3,2,1,0:T(8,128)}, f32[8,512]{1,0:T(8,128)}) custom-call(f32[2,6,8,24,512]{4,3,2,1,0:T(8,128)S(1)} %get-tuple-element.7.state, f32[128,128]{1,0:T(8,128)S(1)} %get-tuple-element.8.incoming, f32[4,8,512]{2,1,0:T(8,128)S(1)} %get-tuple-element.9.finish, ...), custom_call_target="tpu_custom_call" | custom-call | tf_op jit(solution)/shard_map/write/pallas_call | solution.py:585

commit v6 on v5

--- a/solution.py
+++ b/solution.py
@@ -425,6 +425,7 @@
     for turn in range(STEPS):
         for run in range(2):
             boundary(run, turn)
+        for run in range(2):
             if turn < STEPS - 1:
                 interior(run, turn + 1)
             greeted(2 + 2 * turn + run)

time: 43.5 us -> 43.3 us (level)
  Pallas kernels: 41.4 us -> 40.8 us
    pallas_call x1, Pallas kernels: 39.1 us -> 38.6 us  [yee(): pl.pallas_call(yee_kernel, out_shape=(pltpu.VMEM((2, 6) + plane, jnp.floa...]
where the time goes in v6:
time: 43.3 us; the launch traced here: 42.8 us
  Pallas kernels  40.8 us (94%)
  between operations  1.93 us (4%)
    pallas_call x1, Pallas kernels, yee(): pl.pallas_call(yee_kernel, out_shape=(pltpu.VMEM((2, 6) + plane, jnp.floa...  38.6 us
    pallas_call x1, Pallas kernels, yee(): pl.pallas_call(write_kernel, out_shape=(jax.ShapeDtypeStruct(forward.shap...  2.29 us

profile of v6, /device:TPU:1, one launch (start us, length us, event | category | flops | bytes accessed | tf_op | source)
XLA Modules:
  0.0 42.8 jit_solution(18048362175049933167)
XLA Ops:
  1.9 0.1 pad_add_fusion.planes_hbm
  2.0 38.6 %yee.1 = (f32[2,6,8,24,512]{4,3,2,1,0:T(8,128)S(1)}, f32[128,128]{1,0:T(8,128)S(1)}, f32[4,8,512]{2,1,0:T(8,128)S(1)}, f32[15,8,512]{2,1,0:T(8,128)S(1)}) custom-call(f32[8,24,512]{2,1,0:T(8,128)} %inverse_hbm.1, f32[1,6,8,24,512]{4,3,2,1,0:T(8,128)} %forward_hbm.1, f32[1,6,8,24,512]{4,3,2,1,0:T(8,128)} %adjoint_hbm.1, f32[1,3]{1,0:T(1,128)} %swave_hbm.1, ...), custom_call_target="tpu_custom_call" | custom-call | tf_op jit(solution)/shard_map/yee/pallas_call | solution.py:537
  40.6 2.3 %write.1 = (f32[1,6,8,24,512]{4,3,2,1,0:T(8,128)}, f32[1,6,8,24,512]{4,3,2,1,0:T(8,128)}, f32[8,512]{1,0:T(8,128)}) custom-call(f32[2,6,8,24,512]{4,3,2,1,0:T(8,128)S(1)} %get-tuple-element.7.state, f32[128,128]{1,0:T(8,128)S(1)} %get-tuple-element.8.incoming, f32[4,8,512]{2,1,0:T(8,128)S(1)} %get-tuple-element.9.finish, ...), custom_call_target="tpu_custom_call" | custom-call | tf_op jit(solution)/shard_map/write/pallas_call | solution.py:586
